TPU v7x, 256 devices: a whole 4x4x8 slice. The times are simulated.
256 devices in a mesh: blk: 128 (over x, z, y), pipe: 2 (over core).
Axes of the slice: x: 4, y: 4, z: 8, core: 2. Of those that a mesh axis runs over, the one named last changes fastest.
Arguments:
- x_saved: bfloat16 [2, 2, 16384, 4096], P('pipe', None, 'blk'), may hold values from -6 to 6
- cotangent: bfloat16 [2, 16384, 4096], P(None, 'blk'), may hold values from -6 to 6
- seq_right: bfloat16 [2, 128, 128, 128], P('pipe', 'blk'), may hold values from -0.5 to 0.5
- seq_left: bfloat16 [2, 128, 128, 128], P('pipe', 'blk'), may hold values from -0.5 to 0.5
- chan_first: bfloat16 [2, 64, 64, 64], P('pipe'), may hold values from -0.75 to 0.75
- chan_second: bfloat16 [2, 64, 64, 64], P('pipe'), may hold values from -0.75 to 0.75
Outputs:
- grad_input: bfloat16 [2, 2, 16384, 4096], P('pipe', None, 'blk')
- grad_right: float32 [2, 128, 128, 128], P('pipe', 'blk')
- grad_left: float32 [2, 128, 128, 128], P('pipe', 'blk')
- grad_first: float32 [2, 64, 64, 64], P('pipe')
- grad_second: float32 [2, 64, 64, 64], P('pipe')
All inputs are finite; a program needn't handle non-finite values.
Results may differ from a plain program's by a relative error of at most 0.01.
Values may be sent and summed in bfloat16 or wider, within the bound.
A program may use at most 128 MiB of HBM per device.

v0:
```python
import jax
import jax.numpy as jnp
from jax import lax
from jax.sharding import PartitionSpec as P


def shifted(block, axis, distance):
    devices = range(lax.axis_size(axis))
    route = [(i - distance, i) for i in devices if i - distance in devices]
    return lax.ppermute(block, axis, route)


def prepare(activation, right_block, first_block, second_block):
    tokens, width = activation.shape
    act_cols = activation.T.reshape(first_block.shape[0], first_block.shape[2], tokens)
    mixed = jnp.einsum(
        "akj,ajs->aks", first_block, act_cols, preferred_element_type=jnp.float32
    ).astype(jnp.bfloat16)
    mixed_k = jnp.transpose(mixed, (1, 0, 2))
    hidden = jnp.einsum(
        "kma,kas->kms", second_block, mixed_k, preferred_element_type=jnp.float32
    ).astype(jnp.bfloat16)
    hidden_cols = hidden.reshape(width, right_block.shape[0], right_block.shape[2])
    seq_rows = jnp.einsum(
        "ikj,dij->kid", right_block, hidden_cols, preferred_element_type=jnp.float32
    ).astype(jnp.bfloat16)
    return (act_cols, mixed_k, hidden_cols, seq_rows)


def after_rows(activation, grad_out, gathered, left_block):
    tokens, width = activation.shape
    carried = jnp.einsum(
        "kmi,kid->kmd", left_block, gathered, preferred_element_type=jnp.float32
    ).reshape(tokens, width)
    gate_grad = (grad_out.astype(jnp.float32) * activation.astype(jnp.float32)).astype(jnp.bfloat16)
    gate_grad = gate_grad.reshape(left_block.shape[0], left_block.shape[1], width)
    left_grad = jnp.einsum("kmd,kid->kmi", gate_grad, gathered, preferred_element_type=jnp.float32)
    back_rows = jnp.einsum(
        "kmi,kmd->ikd", left_block, gate_grad, preferred_element_type=jnp.float32
    ).astype(jnp.bfloat16)
    return (carried, left_grad, back_rows)


def finish(
    activation,
    grad_out,
    carried,
    returned,
    act_cols,
    mixed_k,
    hidden_cols,
    right_block,
    first_block,
    second_block,
):
    tokens, width = activation.shape
    right_grad = jnp.einsum(
        "ikd,dij->ikj", returned, hidden_cols, preferred_element_type=jnp.float32
    )
    hidden_grad = jnp.einsum(
        "ikj,ikd->dij", right_block, returned, preferred_element_type=jnp.float32
    ).astype(jnp.bfloat16)
    hidden_grad = hidden_grad.reshape(second_block.shape[0], second_block.shape[1], tokens)
    second_grad = jnp.einsum(
        "kms,kas->kma", hidden_grad, mixed_k, preferred_element_type=jnp.float32
    )
    mixed_grad = jnp.einsum(
        "kma,kms->kas", second_block, hidden_grad, preferred_element_type=jnp.float32
    ).astype(jnp.bfloat16)
    mixed_grad_a = jnp.transpose(mixed_grad, (1, 0, 2))
    first_grad = jnp.einsum(
        "aks,ajs->akj", mixed_grad_a, act_cols, preferred_element_type=jnp.float32
    )
    chan_back = (
        jnp.einsum("akj,aks->ajs", first_block, mixed_grad_a, preferred_element_type=jnp.float32)
        .reshape(width, tokens)
        .T
    )
    input_grad = (grad_out.astype(jnp.float32) * carried + chan_back).astype(jnp.bfloat16)
    return (input_grad, right_grad, first_grad, second_grad)


def body(x_saved, cotangent, seq_right, seq_left, chan_first, chan_second):
    sections = lax.axis_size("pipe")
    section = lax.axis_index("pipe")
    saved = x_saved[0]
    micro = saved.shape[0]
    right_block = seq_right[0]
    left_block = seq_left[0]
    first_block = chan_first[0]
    second_block = chan_second[0]
    rounds = micro + sections - 1
    right_acc = jnp.zeros(right_block.shape, jnp.float32)
    left_acc = jnp.zeros(left_block.shape, jnp.float32)
    first_acc = jnp.zeros(first_block.shape, jnp.float32)
    second_acc = jnp.zeros(second_block.shape, jnp.float32)
    grad_store = jnp.zeros_like(saved)
    received = jnp.zeros_like(cotangent[0])
    for moment in range(rounds):
        position = moment - (sections - 1) + section
        valid = (position >= 0) & (position < micro)
        factor = jnp.where(valid, 1.0, 0.0).astype(jnp.float32)
        activation = lax.dynamic_index_in_dim(
            saved, jnp.clip(position, 0, micro - 1), 0, keepdims=False
        )
        grad_out = jnp.where(section == sections - 1, cotangent[min(moment, micro - 1)], received)
        act_cols, mixed_k, hidden_cols, seq_rows = prepare(
            activation, right_block, first_block, second_block
        )
        gathered = lax.all_to_all(seq_rows, "blk", split_axis=0, concat_axis=1, tiled=True)
        carried, left_grad, back_rows = after_rows(activation, grad_out, gathered, left_block)
        returned = lax.all_to_all(back_rows, "blk", split_axis=0, concat_axis=1, tiled=True)
        results = finish(
            activation,
            grad_out,
            carried,
            returned,
            act_cols,
            mixed_k,
            hidden_cols,
            right_block,
            first_block,
            second_block,
        )
        input_grad, right_grad, first_grad, second_grad = results
        right_acc = right_acc + factor * right_grad
        left_acc = left_acc + factor * left_grad
        first_acc = first_acc + factor * first_grad
        second_acc = second_acc + factor * second_grad
        slot_index = jnp.clip(position, 0, micro - 1)
        previous = lax.dynamic_index_in_dim(grad_store, slot_index, 0, keepdims=False)
        grad_store = lax.dynamic_update_index_in_dim(
            grad_store, jnp.where(valid, input_grad, previous), slot_index, 0
        )
        if moment + 1 < rounds:
            received = shifted(input_grad, "pipe", -1)
    first_total, second_total = lax.psum((first_acc, second_acc), "blk")
    return (
        grad_store[None],
        right_acc[None],
        left_acc[None],
        first_total[None],
        second_total[None],
    )


def solution(mesh):
    in_specs = (
        P("pipe", None, "blk", None),
        P(None, "blk", None),
        P("pipe", "blk", None, None),
        P("pipe", "blk", None, None),
        P("pipe", None, None, None),
        P("pipe", None, None, None),
    )
    out_specs = (
        P("pipe", None, "blk", None),
        P("pipe", "blk", None, None),
        P("pipe", "blk", None, None),
        P("pipe", None, None, None),
        P("pipe", None, None, None),
    )
    return jax.shard_map(body, mesh=mesh, in_specs=in_specs, out_specs=out_specs, check_vma=False)
```

profile of v0, /device:TPU:32, one launch (start us, length us, event | category | flops | bytes accessed | tf_op | source)
XLA Modules:
  0.0 581.7 jit_solution(16670342025267970263)
XLA Ops:
  10.7 4.0 constant_dynamic-slice_fusion.1
  25.0 15.5 %all-to-all-start.1 = ((bf16[128,2,2048]{2,1,0:T(2,128)(2,1)}), bf16[128,2,2048]{2,1,0:T(2,128)(2,1)}, u32[]{:S(2)}, u32[]{:S(2)}) async-start(bf16[128,2,2048]{2,1,0:T(2,128)(2,1)} %reshape.255), calls=%async_computation.1 | async-start | bytes 2097152 | tf_op jit(solution)/shard_map/all_to_all | solution.py:112
  52.1 18.2 %all-to-all-done.1 = bf16[128,2,2048]{2,1,0:T(2,128)(2,1)} async-done(((bf16[128,2,2048]{2,1,0:T(2,128)(2,1)}), bf16[128,2,2048]{2,1,0:T(2,128)(2,1)}, u32[]{:S(2)}, u32[]{:S(2)}) %all-to-all-start.1) | async-done | bytes 1048608 | tf_op jit(solution)/shard_map/all_to_all | solution.py:112
  70.3 7.8 %all-to-all-start = ((bf16[128,2,2048]{2,1,0:T(2,128)(2,1)}), bf16[128,2,2048]{2,1,0:T(2,128)(2,1)}, u32[]{:S(2)}, u32[]{:S(2)}) async-start(bf16[128,2,2048]{2,1,0:T(2,128)(2,1)} %reshape.257), calls=%async_computation | async-start | bytes 2097152 | tf_op jit(solution)/shard_map/all_to_all | solution.py:110
  83.3 7.5 %reshape.256 = bf16[128,1,4096]{2,1,0:T(2,128)(2,1)} reshape(bf16[128,2,2048]{2,1,0:T(2,128)(2,1)} %all-to-all-done.1) | data formatting | bytes 2097152
  98.8 8.2 %all-to-all-done = bf16[128,2,2048]{2,1,0:T(2,128)(2,1)} async-done(((bf16[128,2,2048]{2,1,0:T(2,128)(2,1)}), bf16[128,2,2048]{2,1,0:T(2,128)(2,1)}, u32[]{:S(2)}, u32[]{:S(2)}) %all-to-all-start) | async-done | bytes 1048608 | tf_op jit(solution)/shard_map/all_to_all | solution.py:110
  107.0 7.5 %reshape.258 = bf16[128,1,4096]{2,1,0:T(2,128)(2,1)} reshape(bf16[128,2,2048]{2,1,0:T(2,128)(2,1)} %all-to-all-done) | data formatting | bytes 2097152
  114.5 4.7 fusion.6
  128.6 8.0 %all-to-all-start.2 = ((bf16[128,2,2048]{2,1,0:T(2,128)(2,1)}), bf16[128,2,2048]{2,1,0:T(2,128)(2,1)}, u32[]{:S(2)}, u32[]{:S(2)}) async-start(bf16[128,2,2048]{2,1,0:T(2,128)(2,1)} %reshape.261), calls=%async_computation.2 | async-start | bytes 2097152 | tf_op jit(solution)/shard_map/all_to_all | solution.py:110
  151.9 14.2 %all-to-all-done.2 = bf16[128,2,2048]{2,1,0:T(2,128)(2,1)} async-done(((bf16[128,2,2048]{2,1,0:T(2,128)(2,1)}), bf16[128,2,2048]{2,1,0:T(2,128)(2,1)}, u32[]{:S(2)}, u32[]{:S(2)}) %all-to-all-start.2) | async-done | bytes 1048608 | tf_op jit(solution)/shard_map/all_to_all | solution.py:110
  166.1 8.4 %all-to-all-start.3 = ((bf16[128,2,2048]{2,1,0:T(2,128)(2,1)}), bf16[128,2,2048]{2,1,0:T(2,128)(2,1)}, u32[]{:S(2)}, u32[]{:S(2)}) async-start(bf16[128,2,2048]{2,1,0:T(2,128)(2,1)} %reshape.259), calls=%async_computation.3 | async-start | bytes 2097152 | tf_op jit(solution)/shard_map/all_to_all | solution.py:112
  193.7 11.2 %all-to-all-done.3 = bf16[128,2,2048]{2,1,0:T(2,128)(2,1)} async-done(((bf16[128,2,2048]{2,1,0:T(2,128)(2,1)}), bf16[128,2,2048]{2,1,0:T(2,128)(2,1)}, u32[]{:S(2)}, u32[]{:S(2)}) %all-to-all-start.3) | async-done | bytes 1048608 | tf_op jit(solution)/shard_map/all_to_all | solution.py:112
  204.9 7.9 %all-to-all-start.4 = ((bf16[128,2,2048]{2,1,0:T(2,128)(2,1)}), bf16[128,2,2048]{2,1,0:T(2,128)(2,1)}, u32[]{:S(2)}, u32[]{:S(2)}) async-start(bf16[128,2,2048]{2,1,0:T(2,128)(2,1)} %reshape.265), calls=%async_computation.4 | async-start | bytes 2097152 | tf_op jit(solution)/shard_map/all_to_all | solution.py:110
  216.1 7.5 %reshape.262 = bf16[128,1,4096]{2,1,0:T(2,128)(2,1)} reshape(bf16[128,2,2048]{2,1,0:T(2,128)(2,1)} %all-to-all-done.2) | data formatting | bytes 2097152
  225.9 7.5 %reshape.260 = bf16[128,1,4096]{2,1,0:T(2,128)(2,1)} reshape(bf16[128,2,2048]{2,1,0:T(2,128)(2,1)} %all-to-all-done.3) | data formatting | bytes 2097152
  247.9 7.5 %reshape.266 = bf16[128,1,4096]{2,1,0:T(2,128)(2,1)} reshape(bf16[128,2,2048]{2,1,0:T(2,128)(2,1)} %all-to-all-done.4) | data formatting | bytes 2097152
  255.4 4.3 fusion.74
  275.9 14.2 %all-to-all-start.5 = ((bf16[128,2,2048]{2,1,0:T(2,128)(2,1)}), bf16[128,2,2048]{2,1,0:T(2,128)(2,1)}, u32[]{:S(2)}, u32[]{:S(2)}) async-start(bf16[128,2,2048]{2,1,0:T(2,128)(2,1)} %reshape.263), calls=%async_computation.5 | async-start | bytes 2097152 | tf_op jit(solution)/shard_map/all_to_all | solution.py:112
  295.3 4.2 fusion.68
  303.0 18.1 %all-to-all-done.5 = bf16[128,2,2048]{2,1,0:T(2,128)(2,1)} async-done(((bf16[128,2,2048]{2,1,0:T(2,128)(2,1)}), bf16[128,2,2048]{2,1,0:T(2,128)(2,1)}, u32[]{:S(2)}, u32[]{:S(2)}) %all-to-all-start.5) | async-done | bytes 1048608 | tf_op jit(solution)/shard_map/all_to_all | solution.py:112
  321.1 7.5 %reshape.264 = bf16[128,1,4096]{2,1,0:T(2,128)(2,1)} reshape(bf16[128,2,2048]{2,1,0:T(2,128)(2,1)} %all-to-all-done.5) | data formatting | bytes 2097152
  344.5 3.7 fusion.31
  348.2 3.8 fusion.27
  361.4 208.6 %all-reduce.3.cloned.1.call-done = (f32[1,64,64,64]{3,2,1,0:T(8,128)}, f32[1,64,64,64]{3,2,1,0:T(8,128)}) async-done(((f32[1,64,64,64]{3,2,1,0:T(8,128)}, f32[1,64,64,64]{3,2,1,0:T(8,128)}), (f32[1,64,64,64]{3,2,1,0:T(8,128)}, f32[1,64,64,64]{3,2,1,0:T(8,128)})) %all-reduce.3.cloned.1.call-update) | async-done | bytes 2097168 | tf_op jit(solution)/shard_map/psum | solution.py:137
  (178 shorter events, 157.0 us)
Async XLA Ops:
  7.2 34.7 %copy-start = (bf16[1,64,64,64]{3,2,1,0:T(8,128)(2,1)S(1)}, bf16[1,64,64,64]{3,2,1,0:T(8,128)(2,1)}, u32[]{:S(2)}) copy-start(bf16[1,64,64,64]{3,2,1,0:T(8,128)(2,1)} %param.11) | copy-start | bytes 1572868
  10.7 5.6 copy-start.22
  16.3 24.1 %copy-start.11 = (bf16[1,1,128,4096]{2,3,1,0:T(8,128)(2,1)}, bf16[1,1,128,4096]{2,3,1,0:T(8,128)(2,1)S(1)}, u32[]{:S(2)}) copy-start(bf16[1,1,128,4096]{2,3,1,0:T(8,128)(2,1)S(1)} %copy.120) | copy-start | bytes 3145732
  22.3 18.2 %copy-start.1 = (bf16[1,64,64,64]{3,2,1,0:T(8,128)(2,1)S(1)}, bf16[1,64,64,64]{3,2,1,0:T(8,128)(2,1)}, u32[]{:S(2)}) copy-start(bf16[1,64,64,64]{3,2,1,0:T(8,128)(2,1)} %param.10) | copy-start | bytes 1572868
  25.0 45.3 %all-to-all-start.1 = ((bf16[128,2,2048]{2,1,0:T(2,128)(2,1)}), bf16[128,2,2048]{2,1,0:T(2,128)(2,1)}, u32[]{:S(2)}, u32[]{:S(2)}) async-start(bf16[128,2,2048]{2,1,0:T(2,128)(2,1)} %reshape.255), calls=%async_computation.1 | async-start | bytes 2097152 | tf_op jit(solution)/shard_map/all_to_all | solution.py:112
  70.3 36.7 %all-to-all-start = ((bf16[128,2,2048]{2,1,0:T(2,128)(2,1)}), bf16[128,2,2048]{2,1,0:T(2,128)(2,1)}, u32[]{:S(2)}, u32[]{:S(2)}) async-start(bf16[128,2,2048]{2,1,0:T(2,128)(2,1)} %reshape.257), calls=%async_computation | async-start | bytes 2097152 | tf_op jit(solution)/shard_map/all_to_all | solution.py:110
  98.8 15.7 %copy-start.23 = (bf16[1,128,4096]{1,2,0:T(8,128)(2,1)S(1)}, bf16[1,128,4096]{1,2,0:T(8,128)(2,1)}, u32[]{:S(2)}) copy-start(bf16[1,128,4096]{1,2,0:T(8,128)(2,1)} %copy-done.22) | copy-start | bytes 3145732
  114.5 6.0 %copy-start.36 = (bf16[64,128,64]{1,2,0:T(8,128)(2,1)S(1)}, bf16[64,128,64]{1,2,0:T(8,128)(2,1)}, u32[]{:S(2)}) copy-start(bf16[64,128,64]{1,2,0:T(8,128)(2,1)} %convolution_convert_fusion.11) | copy-start | bytes 3145732
  119.2 20.4 %collective-permute-start = (bf16[128,4096]{0,1:T(8,128)(2,1)}, bf16[128,4096]{0,1:T(8,128)(2,1)}, u32[]{:S(2)}, u32[]{:S(2)}) collective-permute-start(bf16[128,4096]{0,1:T(8,128)(2,1)} %fusion.6), channel_id=1, source_target_pairs={{1,0},{3,2},{5,4},{7,6},{9,8},{11,10},{13,12},{15,14},{17,16},{19,... | collective-permute-start | bytes 3145736 | tf_op jit(solution)/shard_map/ppermute | solution.py:10
  125.9 10.7 %copy-start.45 = (bf16[1,128,4096]{2,1,0:T(8,128)(2,1)S(1)}, bf16[1,128,4096]{2,1,0:T(8,128)(2,1)}, u32[]{:S(2)}) copy-start(bf16[1,128,4096]{2,1,0:T(8,128)(2,1)} %get-tuple-element.10) | copy-start | bytes 3145732
  128.6 37.5 %all-to-all-start.2 = ((bf16[128,2,2048]{2,1,0:T(2,128)(2,1)}), bf16[128,2,2048]{2,1,0:T(2,128)(2,1)}, u32[]{:S(2)}, u32[]{:S(2)}) async-start(bf16[128,2,2048]{2,1,0:T(2,128)(2,1)} %reshape.261), calls=%async_computation.2 | async-start | bytes 2097152 | tf_op jit(solution)/shard_map/all_to_all | solution.py:110
  166.1 38.8 %all-to-all-start.3 = ((bf16[128,2,2048]{2,1,0:T(2,128)(2,1)}), bf16[128,2,2048]{2,1,0:T(2,128)(2,1)}, u32[]{:S(2)}, u32[]{:S(2)}) async-start(bf16[128,2,2048]{2,1,0:T(2,128)(2,1)} %reshape.259), calls=%async_computation.3 | async-start | bytes 2097152 | tf_op jit(solution)/shard_map/all_to_all | solution.py:112
  204.9 43.0 %all-to-all-start.4 = ((bf16[128,2,2048]{2,1,0:T(2,128)(2,1)}), bf16[128,2,2048]{2,1,0:T(2,128)(2,1)}, u32[]{:S(2)}, u32[]{:S(2)}) async-start(bf16[128,2,2048]{2,1,0:T(2,128)(2,1)} %reshape.265), calls=%async_computation.4 | async-start | bytes 2097152 | tf_op jit(solution)/shard_map/all_to_all | solution.py:110
  240.1 4.2 copy-start.35
  240.1 4.2 copy-start.40
  242.6 21.3 %collective-permute-start.1 = (bf16[128,4096]{0,1:T(8,128)(2,1)}, bf16[128,4096]{0,1:T(8,128)(2,1)}, u32[]{:S(2)}, u32[]{:S(2)}) collective-permute-start(bf16[128,4096]{0,1:T(8,128)(2,1)} %fusion.7), channel_id=1, source_target_pairs={{1,0},{3,2},{5,4},{7,6},{9,8},{11,10},{13,12},{15,14},{17,16},{19,... | collective-permute-start | bytes 3145736 | tf_op jit(solution)/shard_map/ppermute | solution.py:10
  255.4 4.3 copy-start.12
  255.4 4.3 copy-start.25
  275.9 45.2 %all-to-all-start.5 = ((bf16[128,2,2048]{2,1,0:T(2,128)(2,1)}), bf16[128,2,2048]{2,1,0:T(2,128)(2,1)}, u32[]{:S(2)}, u32[]{:S(2)}) async-start(bf16[128,2,2048]{2,1,0:T(2,128)(2,1)} %reshape.263), calls=%async_computation.5 | async-start | bytes 2097152 | tf_op jit(solution)/shard_map/all_to_all | solution.py:112
  290.2 279.8 %all-reduce.3.cloned.1.call-start = ((), (), s32[]{:S(2)}) async-start(), calls=%async_computation.6 | async-start | bytes 8388608 | tf_op jit(solution)/shard_map/psum | solution.py:137
  295.3 4.3 copy-start.5
  295.3 4.3 copy-start.27
  344.4 3.7 copy-start.10
  348.2 3.8 copy-start.18
  (34 other events, 65.3 us)
Sparse Core Ops, SparseCore 0:
  339.8 230.1 all-reduce.2
where the time goes:
time: 593 us; the launch traced here: 582 us
  waiting for transfers between devices  278 us (47%)
  local copies, waits for them, and re-layouts  125 us (21%)
  matrix products  74.1 us (12%)
  starting transfers between devices  65 us (11%)
  other arithmetic  24.8 us (4%)
  between operations  14.8 us (2%)
    psum x1, waiting for transfers between devices, body(): first_total, second_total = lax.psum((first_acc, second_acc), 'blk')  209 us
    unnamed x121, local copies, waits for them, and re-layouts  94.1 us
    all_to_all x3, waiting for transfers between devices, body(): lax.all_to_all(back_rows, 'blk', split_axis=0, concat_axis=1, tiled=True)  47.5 us
    all_to_all x3, starting transfers between devices, body(): lax.all_to_all(back_rows, 'blk', split_axis=0, concat_axis=1, tiled=True)  38.1 us
    all_to_all x3, starting transfers between devices, body(): lax.all_to_all(seq_rows, 'blk', split_axis=0, concat_axis=1, tiled=True)  23.6 us
    all_to_all x3, waiting for transfers between devices, body(): lax.all_to_all(seq_rows, 'blk', split_axis=0, concat_axis=1, tiled=True)  22.3 us
  transfers between devices with their start and end apart: 9, of which 6 were waited for; matrix products, arithmetic and copies ran while one was open for 25% of the time, Pallas kernels for 0%

commit v1 on v0

v1 whole, which is shorter than its diff:
```python
import functools

import jax
import jax.numpy as jnp
from jax import lax
from jax.experimental import pallas as pl
from jax.experimental.pallas import tpu as pltpu
from jax.sharding import PartitionSpec as P

MESH = pl.DeviceIdType.MESH
NX, NZ, NY = 4, 8, 4
NB = NX * NZ * NY


def full_barrier(me):
    barrier = pltpu.get_barrier_semaphore()

    def greet(step, carry):
        peer = lax.rem(me + step, NB)
        pl.semaphore_signal(barrier, inc=1, device_id={"blk": peer}, device_id_type=MESH)
        return carry

    lax.fori_loop(1, NB, greet, 0)
    pl.semaphore_wait(barrier, NB - 1)


def exchange_kernel(count, *refs):
    sources, targets = refs[:count], refs[count : 2 * count]
    send_sem, recv_sem, own_sem = refs[2 * count :]
    me = lax.axis_index("blk")
    full_barrier(me)
    for index in range(count):
        src, dst = sources[index], targets[index]

        def send(step, carry):
            peer = lax.rem(me + step, NB)
            pltpu.make_async_remote_copy(
                src_ref=src.at[peer],
                dst_ref=dst.at[me],
                send_sem=send_sem.at[index],
                recv_sem=recv_sem.at[index],
                device_id={"blk": peer},
                device_id_type=MESH,
            ).start()
            return carry

        lax.fori_loop(1, NB, send, 0)
        own = pltpu.make_async_copy(src.at[me], dst.at[me], own_sem)
        own.start()
        own.wait()
    for index in range(count):
        src, dst = sources[index], targets[index]
        rest = pl.ds(0, NB - 1)
        pltpu.make_async_copy(src.at[rest], dst.at[rest], send_sem.at[index]).wait()
        pltpu.make_async_copy(src.at[rest], dst.at[rest], recv_sem.at[index]).wait()


def exchange(blocks, ident):
    count = len(blocks)
    width = blocks[0].shape[-1]
    shaped = [b.reshape(NB, width // 128, 128) for b in blocks]
    outs = pl.pallas_call(
        functools.partial(exchange_kernel, count),
        name=f"exchange_{ident}",
        out_shape=[jax.ShapeDtypeStruct(s.shape, s.dtype) for s in shaped],
        in_specs=[pl.BlockSpec(memory_space=pltpu.VMEM)] * count,
        out_specs=[pl.BlockSpec(memory_space=pltpu.VMEM)] * count,
        scratch_shapes=[
            pltpu.SemaphoreType.DMA((count,)),
            pltpu.SemaphoreType.DMA((count,)),
            pltpu.SemaphoreType.DMA,
        ],
        compiler_params=pltpu.CompilerParams(
            collective_id=ident, has_side_effects=True, vmem_limit_bytes=32 << 20
        ),
    )(*shaped)
    return [o.reshape(NB, width) for o in outs]


def reduce_kernel(a_ref, o_ref, sx, rx, ax, sy, ry, ay, sz, rz, gz, gy, gx, send_sem, recv_sem):
    me = lax.axis_index("blk")
    x, z, y = lax.div(me, NZ * NY), lax.rem(lax.div(me, NY), NZ), lax.rem(me, NY)

    def at(px, pz, py):
        return {"blk": (px * NZ + pz) * NY + py}

    peers = []
    for d in range(1, NX):
        peers.append((at(lax.rem(x + d, NX), z, y), at(lax.rem(x + NX - d, NX), z, y)))
    for d in range(1, NY):
        peers.append((at(x, z, lax.rem(y + d, NY)), at(x, z, lax.rem(y + NY - d, NY))))
    for d in range(1, NZ):
        peers.append((at(x, lax.rem(z + d, NZ), y), at(x, lax.rem(z + NZ - d, NZ), y)))
    barrier = pltpu.get_barrier_semaphore()
    for to, _ in peers:
        pl.semaphore_signal(barrier, inc=1, device_id=to, device_id_type=MESH)
    pl.semaphore_wait(barrier, len(peers))

    slot = [0]

    def scatter(values, coord, size, stage, landing, base):
        rows = landing.shape[1]
        copies = []
        for d in range(1, size):
            owner = lax.rem(coord + d, size)
            copy = pltpu.make_async_remote_copy(
                src_ref=stage.at[pl.ds(pl.multiple_of(owner * rows, rows), rows)],
                dst_ref=landing.at[d],
                send_sem=send_sem.at[base + d],
                recv_sem=recv_sem.at[base + d],
                device_id=peers[base + d - 1][0],
                device_id_type=MESH,
            )
            copy.start()
            copies.append(copy)
        for copy in copies:
            copy.wait()
        total = values[pl.ds(pl.multiple_of(coord * rows, rows), rows), :]
        for d in range(1, size):
            total = total + landing[d].astype(jnp.float32)
        return total

    def gather(coord, size, src, landing, base, sem_base):
        copies = []
        for d in range(1, size):
            copy = pltpu.make_async_remote_copy(
                src_ref=src,
                dst_ref=landing.at[coord],
                send_sem=send_sem.at[sem_base + d],
                recv_sem=recv_sem.at[sem_base + d],
                device_id=peers[base + d - 1][0],
                device_id_type=MESH,
            )
            copy.start()
            copies.append(copy)
        for copy in copies:
            copy.wait()

    sx[...] = a_ref[...].astype(jnp.bfloat16)
    ax[...] = scatter(a_ref, x, NX, sx, rx, 0)
    sy[...] = ax[...].astype(jnp.bfloat16)
    ay[...] = scatter(ax, y, NY, sy, ry, NX - 1)
    sz[...] = ay[...].astype(jnp.bfloat16)
    zb = NX + NY - 2
    result = scatter(ay, z, NZ, sz, rz, zb).astype(jnp.bfloat16)
    gz[z] = result
    count = NX + NY + NZ - 3
    gather(z, NZ, gz.at[z], gz, zb, count + zb)
    mid = gz[...]
    gy[y] = mid
    gather(y, NY, gy.at[y], gy, NX - 1, count + NX - 1)
    gx[x] = gy[...]
    gather(x, NX, gx.at[x], gx, 0, count)
    o_ref[...] = gx[...].astype(jnp.float32).reshape(o_ref.shape)


def reduce_all(values, ident):
    rows = values.shape[0]
    rx, ry, rz = rows // NX, rows // NX // NY, rows // NB
    f32, bf16 = jnp.float32, jnp.bfloat16
    n_sem = 2 * (NX + NY + NZ - 3) + 1
    return pl.pallas_call(
        reduce_kernel,
        name=f"reduce_{ident}",
        out_shape=jax.ShapeDtypeStruct(values.shape, f32),
        in_specs=[pl.BlockSpec(memory_space=pltpu.VMEM)],
        out_specs=pl.BlockSpec(memory_space=pltpu.VMEM),
        scratch_shapes=[
            pltpu.VMEM((rows, 128), bf16),
            pltpu.VMEM((NX, rx, 128), bf16),
            pltpu.VMEM((rx, 128), f32),
            pltpu.VMEM((rx, 128), bf16),
            pltpu.VMEM((NY, ry, 128), bf16),
            pltpu.VMEM((ry, 128), f32),
            pltpu.VMEM((ry, 128), bf16),
            pltpu.VMEM((NZ, rz, 128), bf16),
            pltpu.VMEM((NZ, rz, 128), bf16),
            pltpu.VMEM((NY, NZ, rz, 128), bf16),
            pltpu.VMEM((NX, NY, NZ, rz, 128), bf16),
            pltpu.SemaphoreType.DMA((n_sem,)),
            pltpu.SemaphoreType.DMA((n_sem,)),
        ],
        compiler_params=pltpu.CompilerParams(
            collective_id=ident, has_side_effects=True, vmem_limit_bytes=40 << 20
        ),
    )(values)


def dot(spec, a, b):
    return jnp.einsum(spec, a, b, preferred_element_type=jnp.float32)


def forward(act, right, first, second):
    bf16 = jnp.bfloat16
    width = act.shape[1]
    cols = act.T.reshape(first.shape[0], first.shape[2], act.shape[0])
    mixed = dot("akj,ajs->aks", first, cols).astype(bf16)
    mixed_k = jnp.transpose(mixed, (1, 0, 2))
    hidden = dot("kma,kas->kms", second, mixed_k).astype(bf16).reshape(width, -1)
    rows = dot("kj,dj->kd", right, hidden).astype(bf16)
    return cols, mixed_k, hidden, rows


def gate(act, grad_out, left):
    f32, bf16 = jnp.float32, jnp.bfloat16
    gate_grad = (grad_out.astype(f32) * act.astype(f32)).astype(bf16)
    back = dot("mi,md->id", left, gate_grad).astype(bf16)
    return gate_grad, back


def finish(gate_grad, grad_out, gathered, returned, cols, mixed_k, hidden, weights):
    right, left, first, second = weights
    f32, bf16 = jnp.float32, jnp.bfloat16
    tokens, width = grad_out.shape
    carried = dot("mi,id->md", left, gathered)
    left_grad = dot("md,id->mi", gate_grad, gathered)
    right_grad = dot("kd,dj->kj", returned, hidden)
    hidden_grad = dot("kj,kd->dj", right, returned).astype(bf16)
    hidden_grad = hidden_grad.reshape(second.shape[0], second.shape[1], tokens)
    second_grad = dot("kms,kas->kma", hidden_grad, mixed_k)
    mixed_grad = dot("kma,kms->kas", second, hidden_grad).astype(bf16)
    mixed_grad = jnp.transpose(mixed_grad, (1, 0, 2))
    first_grad = dot("aks,ajs->akj", mixed_grad, cols)
    chan_back = dot("akj,aks->ajs", first, mixed_grad).reshape(width, tokens).T
    input_grad = (grad_out.astype(f32) * carried + chan_back).astype(bf16)
    return input_grad, right_grad, left_grad, first_grad, second_grad


def body(x_saved, cotangent, seq_right, seq_left, chan_first, chan_second):
    core = lax.axis_index("pipe")
    low = core == 0

    def swap(value):
        return lax.ppermute(value, "pipe", [(0, 1), (1, 0)])

    def pick(pair, index):
        return lax.dynamic_index_in_dim(pair, index, 0, keepdims=False)

    saved = x_saved[0]
    mine = (pick(saved, core), seq_right[0, 0], seq_left[0, 0], chan_first[0], chan_second[0])
    theirs = tuple(
        swap(v) for v in (pick(saved, 1 - core), seq_right[0, 0], seq_left[0, 0], chan_first[0], chan_second[0])
    )
    upper = [jnp.where(low, t, m) for m, t in zip(mine, theirs)]
    lower = [jnp.where(low, m, t) for m, t in zip(mine, theirs)]
    grad_out = pick(cotangent, core)

    act1, w1 = upper[0], upper[1:]
    act0, w0 = lower[0], lower[1:]
    cols1, mixed1, hidden1, rows1 = forward(act1, w1[0], w1[2], w1[3])
    gate1, back1 = gate(act1, grad_out, w1[1])
    cols0, mixed0, hidden0, rows0 = forward(act0, w0[0], w0[2], w0[3])
    gathered1, returned1, gathered0 = exchange([rows1, back1, rows0], 1)
    res1 = finish(gate1, grad_out, gathered1, returned1, cols1, mixed1, hidden1, w1)
    grad_mid = res1[0]
    gate0, back0 = gate(act0, grad_mid, w0[1])
    (returned0,) = exchange([back0], 2)
    res0 = finish(gate0, grad_mid, gathered0, returned0, cols0, mixed0, hidden0, w0)

    own = [jnp.where(low, b, a) for a, b in zip(res1, res0)]
    other = [swap(jnp.where(low, a, b)) for a, b in zip(res1, res0)]
    grad_input = jnp.stack([jnp.where(low, own[0], other[0]), jnp.where(low, other[0], own[0])])
    right_grad, left_grad, first_grad, second_grad = [a + b for a, b in zip(own[1:], other[1:])]
    flat = jnp.concatenate([first_grad.reshape(-1, 128), second_grad.reshape(-1, 128)])
    total = reduce_all(flat, 3)
    half = flat.shape[0] // 2
    first_total = total[:half].reshape(first_grad.shape)
    second_total = total[half:].reshape(second_grad.shape)
    return (
        grad_input[None],
        right_grad[None, None],
        left_grad[None, None],
        first_total[None],
        second_total[None],
    )


def solution(mesh):
    in_specs = (
        P("pipe", None, "blk", None),
        P(None, "blk", None),
        P("pipe", "blk", None, None),
        P("pipe", "blk", None, None),
        P("pipe", None, None, None),
        P("pipe", None, None, None),
    )
    out_specs = (
        P("pipe", None, "blk", None),
        P("pipe", "blk", None, None),
        P("pipe", "blk", None, None),
        P("pipe", None, None, None),
        P("pipe", None, None, None),
    )
    return jax.shard_map(body, mesh=mesh, in_specs=in_specs, out_specs=out_specs, check_vma=False)
```

time: 593 us -> 249 us (0.42); the launches traced: 582 us -> 249 us
  waiting for transfers between devices: 278 us -> 1.68 us
  Pallas kernels: 0 us -> 165 us
  local copies, waits for them, and re-layouts: 125 us -> 22.8 us
  starting transfers between devices: 65 us -> 2.66 us
  matrix products: 74.1 us -> 41.2 us
  between operations: 14.8 us -> 1.15 us
  other arithmetic: 24.8 us -> 14.4 us
    psum x1 -> x0, waiting for transfers between devices: 209 us -> none  [body(): first_total, second_total = lax.psum((first_acc, second_acc), 'blk')]
    pallas_call x0 -> x3, Pallas kernels: none -> 165 us  [the longest x2 115 us: exchange(): pl.pallas_call(functools.partial(exchange_kernel, count), name=f'exchange...]
    unnamed x121 -> x76, local copies, waits for them, and re-layouts: 94.1 us -> 6.25 us
    all_to_all x6 -> x0, waiting for transfers between devices: 69.8 us -> none  [the longest x3 47.5 us: body(): lax.all_to_all(back_rows, 'blk', split_axis=0, concat_axis=1, tiled=True)]
    all_to_all x6 -> x0, starting transfers between devices: 61.8 us -> none  [the longest x3 38.1 us: body(): lax.all_to_all(back_rows, 'blk', split_axis=0, concat_axis=1, tiled=True)]
    dot_general x36 -> x24, matrix products: 74.1 us -> 41.2 us  [dot(): return jnp.einsum(spec, a, b, preferred_element_type=jnp.float32)]
    convert_element_type x6 -> x0, other arithmetic: 18 us -> none  [the longest x3 9.32 us: after_rows(): back_rows = jnp.einsum('kmi,kmd->ikd', left_block, gate_grad, preferred_e...]
    dynamic_slice x7 -> x0, local copies, waits for them, and re-layouts: 16.6 us -> none  [the longest x4 9.34 us: body(): lax.dynamic_index_in_dim(grad_store, slot_index, 0, keepdims=False)]
  transfers between devices with their start and end apart: 9 -> 10, of which waited for: 6 -> 1; matrix products, arithmetic and copies ran while one was open for 25% -> 19% of each run, Pallas kernels for 0% -> 20%
where the time goes in v1:
time: 249 us
  Pallas kernels  165 us (66%)
  matrix products  41.2 us (17%)
  local copies, waits for them, and re-layouts  22.8 us (9%)
  other arithmetic  14.4 us (6%)
  starting transfers between devices  2.66 us (1%)
    pallas_call x2, Pallas kernels, exchange(): pl.pallas_call(functools.partial(exchange_kernel, count), name=f'exchange...  115 us
    pallas_call x1, Pallas kernels, reduce_all(): pl.pallas_call(reduce_kernel, name=f'reduce_{ident}', out_shape=jax.Shape...  50.1 us
    dot_general x24, matrix products, dot(): return jnp.einsum(spec, a, b, preferred_element_type=jnp.float32)  41.2 us
    unnamed x76, local copies, waits for them, and re-layouts  6.25 us
    add x2, other arithmetic, body(): a + b  5.77 us
    reshape x2, local copies, waits for them, and re-layouts, finish(): chan_back = dot('akj,aks->ajs', first, mixed_grad).reshape(width, tokens).T  5.76 us
  transfers between devices with their start and end apart: 10, of which 1 were waited for; matrix products, arithmetic and copies ran while one was open for 19% of the time, Pallas kernels for 20%

profile of v1, /device:TPU:32, one launch (start us, length us, event | category | flops | bytes accessed | tf_op | source)
XLA Modules:
  0.0 248.7 jit_solution(15179464438192966346)
XLA Ops:
  3.3 1.7 collective-permute-done.4
  4.9 2.6 %bitcast_select_fusion = (bf16[128,4096]{1,0:T(8,128)(2,1)}, bf16[128,4096]{1,0:T(8,128)(2,1)S(1)}) fusion(bf16[128,4096]{1,0:T(8,128)(2,1)} %collective-permute-done.4, pred[]{:T(512)S(6)} %eq.3, bf16[1,2,128,4096]{3,2,1,0:T(8,128)(2,1)} %param.6, s32[]{:T(128)S(6)} %select_n.113), kind=kLoop, calls=%fused_computation.46 | loop fusion | flops 1048576 | bytes 4194309 | tf_op jit(solution)/shard_map/jit(_where)/select_n | solution.py:245
  9.0 2.3 fusion.6
  11.4 2.4 convolution_convert_fusion.10
  15.2 2.3 copy.31
  20.3 1.7 fusion.7
  24.5 81.7 %exchange_1.1 = (bf16[128,32,128]{2,1,0:T(8,128)(2,1)S(1)}, bf16[128,32,128]{2,1,0:T(8,128)(2,1)S(1)}, bf16[128,32,128]{2,1,0:T(8,128)(2,1)S(1)}) custom-call(bf16[128,32,128]{2,1,0:T(8,128)(2,1)S(1)} %bitcast.172, bf16[128,32,128]{2,1,0:T(8,128)(2,1)S(1)} %bitcast.171, bf16[128,32,128]{2,1,0:T(8,128)(2,1)S(1)} %bitcast.173), custom_call_target="tpu_custom_call" | custom-call | tf_op jit(solution)/shard_map/exchange_1/pallas_call | solution.py:62
  107.7 4.7 %fusion.40 = f32[64,64,128]{2,1,0:T(8,128)} fusion(bf16[64,64,128]{2,0,1:T(8,128)(2,1)S(1)} %fusion.8, bf16[64,64,64]{2,1,0:T(8,128)(2,1)} %collective-permute-done.3, pred[]{:T(512)S(6)} %eq.3, bf16[1,64,64,64]{3,2,1,0:T(8,128)(2,1)} %param.10), kind=kOutput, calls=%fused_computation.73 | convolution fusion | flops 67371008 | bytes 4194305 | tf_op jit(solution)/shard_map/akj,aks->ajs/dot_general | solution.py:190
  112.4 2.9 %copy.36 = f32[4096,128]{0,1:T(8,128)} copy(f32[4096,128]{1,0:T(8,128)} %bitcast.195) | data formatting | bytes 4194304 | tf_op jit(solution)/shard_map/reshape | solution.py:224
  115.2 2.6 %fusion.2 = bf16[128,4096]{1,0:T(8,128)(2,1)S(1)} fusion(f32[4096,128]{0,1:T(8,128)} %copy.36, bf16[16,8,32,128]{3,2,1,0:T(8,128)(2,1)S(1)} %bitcast.177, bf16[2,128,4096]{2,1,0:T(8,128)(2,1)} %param.7, s32[]{:T(128)S(6)} %select_n.113, bf16[128,128]{1,0:T(8,128)(2,1)S(1)} %collective-permute-done, pred[]{:T(512)S(6)} %eq.3, ...), kind=kOutput, calls=%fused_computation.4 | convolution fusion | flops 136331264 | bytes 5308421 | tf_op jit(solution)/shard_map/mi,id->md/dot_general | solution.py:190
  122.3 32.9 %exchange_2.1 = bf16[128,32,128]{2,1,0:T(8,128)(2,1)S(1)} custom-call(bf16[128,32,128]{2,1,0:T(8,128)(2,1)S(1)} %bitcast.176), custom_call_target="tpu_custom_call" | custom-call | tf_op jit(solution)/shard_map/exchange_2/pallas_call | solution.py:62
  161.7 3.2 %broadcast_select_fusion.1 = (f32[64,64,64]{2,1,0:T(8,128)}, f32[64,64,64]{2,1,0:T(8,128)}) fusion(f32[64,64,64]{2,1,0:T(8,128)S(1)} %fusion.34, pred[]{:T(512)S(6)} %eq.3, bf16[64,64,128]{2,1,0:T(8,128)(2,1)S(1)} %bitcast.186, bf16[64,64,128]{2,0,1:T(8,128)(2,1)S(1)} %copy-done.21), kind=kOutput, calls=%fused_computation.52 | convolution fusion | flops 67371008 | bytes 5242881 | tf_op jit(solution)/shard_map/aks,ajs->akj/dot_general | solution.py:190
  164.9 3.3 %broadcast_select_fusion = (f32[64,64,64]{2,1,0:T(8,128)}, f32[64,64,64]{2,1,0:T(8,128)}) fusion(f32[64,64,64]{2,1,0:T(8,128)S(1)} %fusion.42, pred[]{:T(512)S(6)} %eq.3, bf16[64,64,128]{2,1,0:T(8,128)(2,1)S(1)} %bitcast.184, bf16[64,64,128]{2,0,1:T(8,128)(2,1)S(1)} %copy-done.13), kind=kOutput, calls=%fused_computation.51 | convolution fusion | flops 67371008 | bytes 5242881 | tf_op jit(solution)/shard_map/kms,kas->kma/dot_general | solution.py:190
  168.6 4.0 %fusion.36 = f32[64,64,128]{2,1,0:T(8,128)} fusion(bf16[64,64,128]{2,0,1:T(8,128)(2,1)S(1)} %fusion.9, bf16[64,64,64]{2,1,0:T(8,128)(2,1)} %collective-permute-done.3, pred[]{:T(512)S(6)} %eq.3, bf16[1,64,64,64]{3,2,1,0:T(8,128)(2,1)} %param.10), kind=kOutput, calls=%fused_computation.69 | convolution fusion | flops 67371008 | bytes 4194305 | tf_op jit(solution)/shard_map/akj,aks->ajs/dot_general | solution.py:190
  172.6 2.9 %copy.40 = f32[4096,128]{0,1:T(8,128)} copy(f32[4096,128]{1,0:T(8,128)} %bitcast.194) | data formatting | bytes 4194304 | tf_op jit(solution)/shard_map/reshape | solution.py:224
  175.9 4.5 %broadcast_select_fusion.6 = (bf16[128,4096]{1,0:T(8,128)(2,1)}, bf16[128,4096]{1,0:T(8,128)(2,1)}) fusion(bf16[128,4096]{1,0:T(8,128)(2,1)} %copy-done.10, pred[]{:T(512)S(6)} %eq.3, f32[4096,128]{0,1:T(8,128)} %copy.40, bf16[16,8,32,128]{3,2,1,0:T(8,128)(2,1)S(1)} %bitcast.180, bf16[128,128]{1,0:T(8,128)(2,1)S(1)} %collective-permute-done, ...), kind=kOutput, calls=%fused_computation.57 | convolution fusion | flops 136855552 | bytes 6356993 | tf_op jit(solution)/shard_map/mi,id->md/dot_general | solution.py:190
  180.5 1.5 add_bitcast_fusion.1
  183.5 3.8 %select_add_fusion = f32[64,64,64]{2,1,0:T(8,128)} fusion(f32[64,64,64]{2,1,0:T(8,128)} %collective-permute-done.9, f32[64,64,64]{2,1,0:T(8,128)S(1)} %fusion.42, f32[64,64,64]{2,1,0:T(8,128)S(1)} %copy-done.28, pred[]{:T(512)S(6)} %eq.3), kind=kLoop, calls=%fused_computation.18 | loop fusion | flops 524288 | bytes 4194305 | tf_op jit(solution)/shard_map/add | solution.py:263
  187.3 2.0 select_add_fusion.1
  189.6 1.8 reshape.86
  191.6 50.1 %reduce_3.1 = f32[4096,128]{1,0:T(8,128)S(1)} custom-call(f32[4096,128]{1,0:T(8,128)S(1)} %pad_maximum_fusion.a_ref), custom_call_target="tpu_custom_call" | custom-call | tf_op jit(solution)/shard_map/reduce_3/pallas_call | solution.py:162
  241.9 1.7 broadcast_in_dim_reshape.7
  243.5 1.7 broadcast_in_dim_reshape.6
  247.1 1.5 maximum_bitcast_fusion
  (117 shorter events, 27.8 us)
Async XLA Ops:
  2.1 2.9 %collective-permute-start.4 = (bf16[128,4096]{1,0:T(8,128)(2,1)S(1)}, bf16[128,4096]{1,0:T(8,128)(2,1)}, u32[]{:S(2)}, u32[]{:S(2)}) collective-permute-start(bf16[128,4096]{1,0:T(8,128)(2,1)S(1)} %dynamic-slice_bitcast_fusion), channel_id=1, source_target_pairs={{0,1},{1,0},{2,3},{3,2},{4,5},{5,4},{6,7},{7,6},{8,9},{9,8},{10,11... | collective-permute-start | bytes 3145736 | tf_op jit(solution)/shard_map/ppermute | solution.py:234
  2.2 11.6 %collective-permute-start = (bf16[128,128]{1,0:T(8,128)(2,1)S(1)}, bf16[128,128]{1,0:T(8,128)(2,1)S(1)}, u32[]{:S(2)}, u32[]{:S(2)}) collective-permute-start(bf16[128,128]{1,0:T(8,128)(2,1)S(1)} %bitcast.199), channel_id=1, source_target_pairs={{0,1},{1,0},{2,3},{3,2},{4,5},{5,4},{6,7},{7,6},{8,9},{9,8},{10,11... | collective-permute-start | bytes 98312 | tf_op jit(solution)/shard_map/ppermute | solution.py:234
  2.7 16.4 %collective-permute-start.1 = (bf16[128,128]{1,0:T(8,128)(2,1)S(1)}, bf16[128,128]{1,0:T(8,128)(2,1)S(1)}, u32[]{:S(2)}, u32[]{:S(2)}) collective-permute-start(bf16[128,128]{1,0:T(8,128)(2,1)S(1)} %bitcast.198), channel_id=1, source_target_pairs={{0,1},{1,0},{2,3},{3,2},{4,5},{5,4},{6,7},{7,6},{8,9},{9,8},{10,11... | collective-permute-start | bytes 98312 | tf_op jit(solution)/shard_map/ppermute | solution.py:234
  2.8 8.6 %collective-permute-start.2 = (bf16[64,64,64]{2,1,0:T(8,128)(2,1)S(1)}, bf16[64,64,64]{2,1,0:T(8,128)(2,1)S(1)}, u32[]{:S(2)}, u32[]{:S(2)}) collective-permute-start(bf16[64,64,64]{2,1,0:T(8,128)(2,1)S(1)} %bitcast.181), channel_id=1, source_target_pairs={{0,1},{1,0},{2,3},{3,2},{4,5},{5,4},{6,7},{7,6},{8,9},{9,8},{10,11... | collective-permute-start | bytes 1572872 | tf_op jit(solution)/shard_map/ppermute | solution.py:234
  3.2 5.8 %collective-permute-start.3 = (bf16[64,64,64]{2,1,0:T(8,128)(2,1)}, bf16[64,64,64]{2,1,0:T(8,128)(2,1)}, u32[]{:S(2)}, u32[]{:S(2)}) collective-permute-start(bf16[64,64,64]{2,1,0:T(8,128)(2,1)} %bitcast.4), channel_id=1, source_target_pairs={{0,1},{1,0},{2,3},{3,2},{4,5},{5,4},{6,7},{7,6},{8,9},{9,8},{10,11... | collective-permute-start | bytes 1572872 | tf_op jit(solution)/shard_map/ppermute | solution.py:234
  7.6 6.2 %copy-start.8 = (bf16[128,4096]{1,0:T(8,128)(2,1)}, bf16[128,4096]{1,0:T(8,128)(2,1)S(1)}, u32[]{:S(2)}) copy-start(bf16[128,4096]{1,0:T(8,128)(2,1)S(1)} %get-tuple-element.14) | copy-start | bytes 3145732
  11.4 10.7 %copy-start.5 = (bf16[64,64,64]{2,1,0:T(8,128)(2,1)}, bf16[64,64,64]{2,1,0:T(8,128)(2,1)S(1)}, u32[]{:S(2)}) copy-start(bf16[64,64,64]{2,1,0:T(8,128)(2,1)S(1)} %collective-permute-done.2) | copy-start | bytes 1572868
  15.2 3.8 %copy-start.17 = (bf16[64,64,128]{2,1,0:T(8,128)(2,1)S(1)}, bf16[64,64,128]{2,1,0:T(8,128)(2,1)}, u32[]{:S(2)}) copy-start(bf16[64,64,128]{2,1,0:T(8,128)(2,1)} %convolution_convert_fusion.10) | copy-start | bytes 3145732
  24.4 82.3 %copy-start.3 = (bf16[1,64,64,64]{3,2,1,0:T(8,128)(2,1)S(1)}, bf16[1,64,64,64]{3,2,1,0:T(8,128)(2,1)}, u32[]{:S(2)}) copy-start(bf16[1,64,64,64]{3,2,1,0:T(8,128)(2,1)} %param.11) | copy-start | bytes 1572868
  24.5 82.3 %copy-start.6 = (bf16[64,64,64]{2,1,0:T(8,128)(2,1)S(1)}, bf16[64,64,64]{2,1,0:T(8,128)(2,1)}, u32[]{:S(2)}) copy-start(bf16[64,64,64]{2,1,0:T(8,128)(2,1)} %copy-done.5) | copy-start | bytes 1572868
  107.7 4.7 %copy-start.20 = (bf16[64,64,128]{2,0,1:T(8,128)(2,1)}, bf16[64,64,128]{2,0,1:T(8,128)(2,1)S(1)}, u32[]{:S(2)}) copy-start(bf16[64,64,128]{2,0,1:T(8,128)(2,1)S(1)} %fusion.8) | copy-start | bytes 3145732
  117.8 3.7 %copy-start.10 = (bf16[128,4096]{1,0:T(8,128)(2,1)}, bf16[128,4096]{1,0:T(8,128)(2,1)S(1)}, u32[]{:S(2)}) copy-start(bf16[128,4096]{1,0:T(8,128)(2,1)S(1)} %fusion.2) | copy-start | bytes 3145732
  122.0 33.2 %copy-start.32 = (bf16[64,64,128]{2,1,0:T(8,128)(2,1)S(1)}, bf16[64,64,128]{2,1,0:T(8,128)(2,1)}, u32[]{:S(2)}) copy-start(bf16[64,64,128]{2,1,0:T(8,128)(2,1)} %copy-done.31) | copy-start | bytes 3145732
  122.3 33.5 %copy-start.18 = (bf16[64,64,128]{2,1,0:T(8,128)(2,1)S(1)}, bf16[64,64,128]{2,1,0:T(8,128)(2,1)}, u32[]{:S(2)}) copy-start(bf16[64,64,128]{2,1,0:T(8,128)(2,1)} %convolution_convert_fusion.10) | copy-start | bytes 3145732
  158.8 21.7 %collective-permute-start.6 = (f32[128,128]{1,0:T(8,128)}, f32[128,128]{1,0:T(8,128)}, u32[]{:S(2)}, u32[]{:S(2)}) collective-permute-start(f32[128,128]{1,0:T(8,128)} %get-tuple-element.19), channel_id=1, source_target_pairs={{0,1},{1,0},{2,3},{3,2},{4,5},{5,4},{6,7},{7,6},{8,9},{9,8},{10,11... | collective-permute-start | bytes 196616 | tf_op jit(solution)/shard_map/ppermute | solution.py:234
  158.9 23.1 %collective-permute-start.7 = (f32[128,128]{1,0:T(8,128)}, f32[128,128]{1,0:T(8,128)}, u32[]{:S(2)}, u32[]{:S(2)}) collective-permute-start(f32[128,128]{1,0:T(8,128)} %get-tuple-element.21), channel_id=1, source_target_pairs={{0,1},{1,0},{2,3},{3,2},{4,5},{5,4},{6,7},{7,6},{8,9},{9,8},{10,11... | collective-permute-start | bytes 196616 | tf_op jit(solution)/shard_map/ppermute | solution.py:234
  161.7 3.2 %copy-start.13 = (bf16[64,64,128]{2,0,1:T(8,128)(2,1)S(1)}, bf16[64,64,128]{2,0,1:T(8,128)(2,1)}, u32[]{:S(2)}) copy-start(bf16[64,64,128]{2,0,1:T(8,128)(2,1)} %copy-done.12) | copy-start | bytes 3145732
  161.7 3.2 %copy-start.15 = (bf16[4096,128]{1,0:T(8,128)(2,1)S(1)}, bf16[4096,128]{1,0:T(8,128)(2,1)}, u32[]{:S(2)}) copy-start(bf16[4096,128]{1,0:T(8,128)(2,1)} %copy-done.14) | copy-start | bytes 3145732
  168.2 15.3 %collective-permute-start.9 = (f32[64,64,64]{2,1,0:T(8,128)}, f32[64,64,64]{2,1,0:T(8,128)}, u32[]{:S(2)}, u32[]{:S(2)}) collective-permute-start(f32[64,64,64]{2,1,0:T(8,128)} %get-tuple-element.23), channel_id=1, source_target_pairs={{0,1},{1,0},{2,3},{3,2},{4,5},{5,4},{6,7},{7,6},{8,9},{9,8},{10,11... | collective-permute-start | bytes 3145736 | tf_op jit(solution)/shard_map/ppermute | solution.py:234
  175.5 8.0 %copy-start.28 = (f32[64,64,64]{2,1,0:T(8,128)S(1)}, f32[64,64,64]{2,1,0:T(8,128)}, u32[]{:S(2)}) copy-start(f32[64,64,64]{2,1,0:T(8,128)} %get-tuple-element.24) | copy-start | bytes 3145732
  175.5 11.8 %collective-permute-start.8 = (f32[64,64,64]{2,1,0:T(8,128)}, f32[64,64,64]{2,1,0:T(8,128)S(1)}, u32[]{:S(2)}, u32[]{:S(2)}) collective-permute-start(f32[64,64,64]{2,1,0:T(8,128)} %get-tuple-element.25), channel_id=1, source_target_pairs={{0,1},{1,0},{2,3},{3,2},{4,5},{5,4},{6,7},{7,6},{8,9},{9,8},{10,11... | collective-permute-start | bytes 3145736 | tf_op jit(solution)/shard_map/ppermute | solution.py:234
  180.4 64.8 %collective-permute-start.5 = (bf16[128,4096]{1,0:T(8,128)(2,1)}, bf16[128,4096]{1,0:T(8,128)(2,1)}, u32[]{:S(2)}, u32[]{:S(2)}) collective-permute-start(bf16[128,4096]{1,0:T(8,128)(2,1)} %get-tuple-element.17), channel_id=1, source_target_pairs={{0,1},{1,0},{2,3},{3,2},{4,5},{5,4},{6,7},{7,6},{8,9},{9,8},{10,11... | collective-permute-start | bytes 3145736 | tf_op jit(solution)/shard_map/ppermute | solution.py:234
  183.5 3.8 %copy-start.1 = (f32[64,64,64]{2,1,0:T(8,128)S(1)}, f32[64,64,64]{2,1,0:T(8,128)}, u32[]{:S(2)}) copy-start(f32[64,64,64]{2,1,0:T(8,128)} %copy-done) | copy-start | bytes 3145732
  183.5 3.8 %copy-start.27 = (f32[64,64,64]{2,1,0:T(8,128)S(1)}, f32[64,64,64]{2,1,0:T(8,128)}, u32[]{:S(2)}) copy-start(f32[64,64,64]{2,1,0:T(8,128)} %get-tuple-element.26) | copy-start | bytes 3145732
  (22 other events, 40.2 us)

commit v2 on v0

v2 whole, which is shorter than its diff:
```python
import jax
import jax.numpy as jnp
from jax import lax
from jax.experimental import pallas as pl
from jax.experimental.pallas import tpu as pltpu
from jax.sharding import PartitionSpec as P

MESH = pl.DeviceIdType.MESH
F32, BF16 = jnp.float32, jnp.bfloat16
NX, NZ, NY = 4, 8, 4
NB = NX * NZ * NY
T = 128
D = 4096
HALF = D // 2
NK = 64
TILE = 512
HR = 2048


def mm(a, b, ca=1, cb=0):
    return lax.dot_general(a, b, (((ca,), (cb,)), ((), ())), preferred_element_type=F32)


def aligned(index, size):
    return pl.ds(pl.multiple_of(index * size, size), size)


def kernel(
    x_in, cot_in, right_in, left_in, first_in, second_in,
    gi_out, right_out, left_out, chan_out,
    x_buf, right_buf, left_buf, first_buf, second_buf,
    gy_buf, gi_buf, gate_buf, pair_buf, mt_buf, mk_buf, ht_buf, hg_buf, cb_buf,
    rexp, lexp, lexp_t,
    send_f, recv_f, send_b, recv_b, dummy, acc, tmp,
    grads, sib, stage1, land1, acc1, stage2, land2, acc2, stage3, land3, gz, gy2, gx, swap_buf,
    lr, lr_sib,
    in_sem, ex_sem, cot_sem, a2a_send, a2a_recv, red_send, red_recv,
    gi_loc, gi_send, gi_recv, lr_send, lr_recv, swap_send, swap_recv, out_sem,
):
    me = lax.axis_index("blk")
    core = lax.axis_index("pipe")
    other = 1 - core
    sibling = {"pipe": other}
    px, pz, py = lax.div(me, NZ * NY), lax.rem(lax.div(me, NY), NZ), lax.rem(me, NY)

    local = (
        (x_in.at[core], x_buf), (left_in, left_buf), (right_in, right_buf),
        (first_in, first_buf), (second_in, second_buf),
    )
    for i, (src, dst) in enumerate(local):
        pltpu.make_async_copy(src, dst.at[core], in_sem.at[core, i]).start()
    cot_copy = pltpu.make_async_copy(cot_in.at[core], gy_buf, cot_sem)
    cot_copy.start()

    barrier = pltpu.get_barrier_semaphore()

    def greet(step, carry):
        peer = lax.rem(me + step, NB)
        pl.semaphore_signal(barrier, inc=1, device_id={"blk": peer}, device_id_type=MESH)
        return carry

    pl.semaphore_signal(barrier, inc=1, device_id=sibling, device_id_type=MESH)
    lax.fori_loop(1, NB, greet, 0)
    pl.semaphore_wait(barrier, NB)

    remote = (
        (x_in.at[other], x_buf), (left_in, left_buf), (right_in, right_buf),
        (first_in, first_buf), (second_in, second_buf),
    )
    ex_copies = []
    for i, (src, dst) in enumerate(remote):
        copy = pltpu.make_async_remote_copy(
            src_ref=src, dst_ref=dst.at[core], send_sem=ex_sem.at[i], recv_sem=in_sem.at[core, i],
            device_id=sibling, device_id_type=MESH,
        )
        copy.start()
        ex_copies.append(copy)

    def await_input(section, i):
        ref = (x_buf, left_buf, right_buf, first_buf, second_buf)[i].at[section]
        pltpu.make_async_copy(ref, ref, in_sem.at[section, i]).wait()

    def all_to_all(src, dst, ident, lo, size):
        columns = pl.ds(lo, size)

        def rows(i):
            return pl.ds(pl.multiple_of(2 * i, 2), 2)

        def send(step, carry):
            peer = lax.rem(me + step, NB)
            pltpu.make_async_remote_copy(
                src_ref=src.at[rows(peer), columns], dst_ref=dst.at[rows(me), columns],
                send_sem=a2a_send.at[ident], recv_sem=a2a_recv.at[ident],
                device_id={"blk": peer}, device_id_type=MESH,
            ).start()
            return carry

        lax.fori_loop(1, NB, send, 0)
        pltpu.make_async_copy(
            src.at[rows(me), columns], dst.at[rows(me), columns], a2a_recv.at[ident]
        ).start()
        pltpu.make_async_copy(
            src.at[rows(me), columns], dummy.at[ident, :, columns], a2a_send.at[ident]
        ).start()

    def await_block(ref, sem, ident, lo, size):
        part = ref.at[:, pl.ds(lo, size)]
        pltpu.make_async_copy(part, part, sem.at[ident]).wait()

    def expand(section):
        row = lax.broadcasted_iota(jnp.int32, (2 * T, T), 0)
        col = lax.broadcasted_iota(jnp.int32, (2 * T, T), 1)
        left = left_buf[section]
        for h in range(2):
            spread = (row == 2 * col + h).astype(F32).astype(BF16)
            part = slice(h * T, (h + 1) * T)
            lexp[section, part, :] = mm(left, spread, 1, 1).astype(BF16)
            lexp_t[section, :, part] = mm(spread, left, 1, 1).astype(BF16)

    def expand_right(section):
        row = lax.broadcasted_iota(jnp.int32, (2 * T, T), 0)
        col = lax.broadcasted_iota(jnp.int32, (2 * T, T), 1)
        right = right_buf[section]
        for h in range(2):
            spread = (row == 2 * col + h).astype(F32).astype(BF16)
            part = slice(h * T, (h + 1) * T)
            rexp[section, :, part] = mm(spread, right).astype(BF16)

    def build_pairs(section):
        row = lax.broadcasted_iota(jnp.int32, (NK, T), 0)
        col = lax.broadcasted_iota(jnp.int32, (NK, T), 1)
        twice = ((col == row) | (col == row + NK)).astype(F32).astype(BF16)
        low = lax.broadcasted_iota(jnp.int32, (T, T), 0) < NK
        first_half = lax.broadcasted_iota(jnp.int32, (T, T), 1) < NK

        def step(b, carry):
            rows = aligned(b, T)
            both = mm(first_buf[section, rows, :], twice)
            pair_buf[section, rows, :] = jnp.where(low == first_half, both, 0.0).astype(BF16)
            return carry

        lax.fori_loop(0, NK // 2, step, 0, unroll=4)

    def gate(section, grad_out, sent):
        def step(i, carry):
            cs = aligned(i, TILE)
            for h in range(2):
                wide = pl.ds(pl.multiple_of(i * TILE + h * HALF, TILE), TILE)
                value = grad_out[:, wide].astype(F32) * x_buf[section, :, wide].astype(F32)
                gate_buf[h * T : (h + 1) * T, cs] = value.astype(BF16)
            sent[:, cs] = mm(lexp_t[section], gate_buf[:, cs]).astype(BF16)
            return carry

        lax.fori_loop(0, HALF // TILE, step, 0)

    def swap_blocks(src, dst):
        def step(g, carry):
            block = src[:, pl.ds(pl.multiple_of(g * 16, 16), 16), :]
            dst[aligned(g, 16), :, :] = jnp.swapaxes(block, 0, 1)
            return carry

        lax.fori_loop(0, NK // 16, step, 0)

    def forward(section, sent):
        def mixed(b, carry):
            cols = aligned(b, T)
            out = mm(pair_buf[section, cols, :], x_buf[section, :, cols], 1, 1)
            mt_buf[aligned(b, 2)] = out.astype(BF16).reshape(2, NK, T)
            return carry

        lax.fori_loop(0, NK // 2, mixed, 0, unroll=4)
        swap_blocks(mt_buf, mk_buf.at[section])

        def hidden(k, carry):
            rows = aligned(k, NK)
            for h in range(2):
                kk = k + h * (NK // 2)
                out = mm(second_buf[section, kk], mk_buf[section, kk])
                ht_buf[section, rows, h * T : (h + 1) * T] = out.astype(BF16)
            return carry

        lax.fori_loop(0, NK // 2, hidden, 0, unroll=4)

        def rows_of(i, carry):
            cs = aligned(i, TILE)
            sent[:, cs] = mm(rexp[section], ht_buf[section, cs, :], 1, 1).astype(BF16)
            return carry

        lax.fori_loop(0, HALF // TILE, rows_of, 0)

    def fold(target):
        even = lax.rem(lax.broadcasted_iota(jnp.int32, (2 * T, T), 0), 2) == 0
        tmp[...] = jnp.where(even, acc[:, :T], acc[:, T:])
        target[...] = tmp[pl.ds(0, T, stride=2), :] + tmp[pl.ds(1, T, stride=2), :]

    def channel_back(section, returned):
        acc[...] = jnp.zeros_like(acc)

        def step(i, carry):
            cs = aligned(i, TILE)
            acc[...] += mm(returned[:, cs], ht_buf[section, cs, :])
            hg_buf[cs, :] = mm(returned[:, cs], rexp[section], 0, 0).astype(BF16)
            return carry

        lax.fori_loop(0, HALF // TILE, step, 0)
        fold(lr.at[section, 0])
        first_half = lax.broadcasted_iota(jnp.int32, (NK, T), 1) < NK

        def pair(b, carry):
            for h in range(2):
                k0 = 2 * b + h * (NK // 2)
                grad = hg_buf[aligned(b, T), h * T : (h + 1) * T]
                mix = mk_buf[section, pl.ds(k0, 2)].reshape(T, T)
                outer = mm(grad, mix, 1, 1)
                grads[section, 1, pl.ds(pl.multiple_of(k0 * (NK // 2), NK), NK), :] = jnp.where(
                    first_half, outer[:NK], outer[NK:]
                )
                for q in range(2):
                    back = mm(second_buf[section, k0 + q], grad[q * NK : (q + 1) * NK], 0, 0)
                    mt_buf[k0 + q] = back.astype(BF16)
            return carry

        lax.fori_loop(0, NK // 4, pair, 0, unroll=2)
        swap_blocks(mt_buf, mg_view)

        def columns(b, carry):
            cols = aligned(b, T)
            mixed_grad = mg_view[aligned(b, 2)].reshape(T, T)
            outer = mm(mixed_grad, x_buf[section, :, cols])
            grads[section, 0, aligned(b, NK), :] = jnp.where(first_half, outer[:NK], outer[NK:])
            cb_buf[:, cols] = mm(mixed_grad, pair_buf[section, cols, :], 0, 0)
            return carry

        lax.fori_loop(0, NK // 2, columns, 0, unroll=4)

    mg_view = mk_buf.at[2]

    def carry_out(section, gathered, grad_out, lo, size):
        def step(i, carry):
            off = lo + i * TILE
            cs = pl.ds(pl.multiple_of(off, TILE), TILE)
            block = gathered[:, cs]
            carried = mm(lexp[section], block)
            for h in range(2):
                wide = pl.ds(pl.multiple_of(off + h * HALF, TILE), TILE)
                value = grad_out[:, wide].astype(F32) * carried[h * T : (h + 1) * T] + cb_buf[:, wide]
                gi_buf[section, :, wide] = value.astype(BF16)
            acc[...] += mm(block, gate_buf[:, cs], 1, 1)
            return carry

        lax.fori_loop(0, size // TILE, step, 0)

    def finish_left(section):
        fold(tmp2)
        lr[section, 1] = tmp2[...].T

    tmp2 = acc2.at[2]

    def send_input_grad(section):
        @pl.when(core == section)
        def _():
            pltpu.make_async_copy(gi_buf.at[section], gi_out.at[core], gi_loc).start()

        @pl.when(core != section)
        def _():
            pltpu.make_async_remote_copy(
                src_ref=gi_buf.at[section], dst_ref=gi_out.at[core], send_sem=gi_send, recv_sem=gi_recv,
                device_id=sibling, device_id_type=MESH,
            ).start()

    is_low = core == 0
    coord1, coord2 = jnp.where(is_low, px, py), jnp.where(is_low, py, px)
    stride1, stride2 = jnp.where(is_low, NZ * NY, 1), jnp.where(is_low, 1, NZ * NY)
    axes = ((coord1, stride1, NX), (coord2, stride2, NY), (pz, NY, NZ))

    def hop(axis, d):
        coord, stride, size = axes[axis]
        return {"blk": me + (lax.rem(coord + d, size) - coord) * stride}

    def copies(section, base, axis, src_of, dst_of):
        size = axes[axis][2]
        return [
            pltpu.make_async_remote_copy(
                src_ref=src_of(d), dst_ref=dst_of(d),
                send_sem=red_send.at[section, base + d], recv_sem=red_recv.at[section, base + d],
                device_id=hop(axis, d), device_id_type=MESH,
            )
            for d in range(1, size)
        ]

    def scatter(section, base, axis, stage, landing):
        coord, _, size = axes[axis]
        rows = landing.shape[2]
        return copies(
            section, base, axis,
            lambda d: stage.at[section, aligned(lax.rem(coord + d, size), rows)],
            lambda d: landing.at[section, d],
        )

    def gather(section, base, axis, buf):
        coord = axes[axis][0]
        return copies(
            section, base, axis,
            lambda d: buf.at[section, coord],
            lambda d: buf.at[section, coord],
        )

    def sib_copy(section):
        return pltpu.make_async_remote_copy(
            src_ref=grads.at[section, other], dst_ref=sib.at[section],
            send_sem=red_send.at[section, 0], recv_sem=red_recv.at[section, 0],
            device_id=sibling, device_id_type=MESH,
        )

    def start(group):
        for c in group:
            c.start()

    def finish(group):
        for c in group:
            c.wait()

    def reduce_stage(section, number):
        def s1():
            return scatter(section, 0, 0, stage1, land1)

        def s2():
            return scatter(section, 3, 1, stage2, land2)

        def s3():
            return scatter(section, 6, 2, stage3, land3)

        def g3():
            return gather(section, 13, 2, gz)

        def g2():
            return gather(section, 20, 1, gy2)

        def g1():
            return gather(section, 23, 0, gx)

        def settle(values, coord, landing, size):
            rows = landing.shape[2]
            total = values[aligned(coord, rows), :]
            for d in range(1, size):
                total = total + landing[section, d].astype(F32)
            return total

        if number == 0:
            sib_copy(section).start()
        elif number == 1:
            sib_copy(section).wait()
            mine = grads.at[section, core]

            def add(i, carry):
                rows = aligned(i, 256)
                total = mine[rows, :] + sib[section, rows, :]
                sib[section, rows, :] = total
                stage1[section, rows, :] = total.astype(BF16)
                return carry

            lax.fori_loop(0, HR // 256, add, 0)
            start(s1())
        elif number == 2:
            finish(s1())
            value = settle(sib.at[section], coord1, land1, NX)
            acc1[section] = value
            stage2[section] = value.astype(BF16)
            start(s2())
        elif number == 3:
            finish(s2())
            value = settle(acc1.at[section], coord2, land2, NY)
            acc2[section] = value
            stage3[section] = value.astype(BF16)
            start(s3())
        elif number == 4:
            finish(s3())
            value = settle(acc2.at[section], pz, land3, NZ)
            gz[section, pz] = value.astype(BF16)
            start(g3())
        elif number == 5:
            finish(g3())
            gy2[section, coord2] = gz[section].reshape(T, T)
            start(g2())
        elif number == 6:
            finish(g2())
            gx[section, coord1] = gy2[section].reshape(NY * T, T)
            start(g1())
        else:
            finish(g1())

    cot_copy.wait()
    await_input(1, 1)
    expand(1)
    await_input(1, 0)
    gate(1, gy_buf, send_b.at[1])
    all_to_all(send_b.at[1], recv_b.at[1], 0, 0, HALF)

    await_input(1, 2)
    expand_right(1)
    await_input(1, 3)
    build_pairs(1)
    await_input(1, 4)
    forward(1, send_f.at[1])
    all_to_all(send_f.at[1], recv_f.at[1], 1, 0, HALF)

    for i in range(5):
        await_input(0, i)
    expand(0)
    expand_right(0)
    build_pairs(0)
    forward(0, send_f.at[0])
    all_to_all(send_f.at[0], recv_f.at[0], 2, 0, HALF // 2)

    await_block(recv_b.at[1], a2a_recv, 0, 0, HALF)
    channel_back(1, recv_b.at[1])
    reduce_stage(1, 0)
    reduce_stage(1, 1)

    await_block(recv_f.at[1], a2a_recv, 1, 0, HALF)
    acc[...] = jnp.zeros_like(acc)
    carry_out(1, recv_f.at[1], gy_buf, 0, HALF)
    finish_left(1)
    gate(0, gi_buf.at[1], send_b.at[0])
    all_to_all(send_b.at[0], recv_b.at[0], 3, 0, HALF)
    all_to_all(send_f.at[0], recv_f.at[0], 4, HALF // 2, HALF // 2)
    send_input_grad(1)
    for number in range(2, 8):
        reduce_stage(1, number)

    await_block(recv_b.at[0], a2a_recv, 3, 0, HALF)
    channel_back(0, recv_b.at[0])
    reduce_stage(0, 0)
    reduce_stage(0, 1)
    await_block(recv_f.at[0], a2a_recv, 2, 0, HALF // 2)
    acc[...] = jnp.zeros_like(acc)
    carry_out(0, recv_f.at[0], gi_buf.at[1], 0, HALF // 2)
    reduce_stage(0, 2)
    await_block(recv_f.at[0], a2a_recv, 4, HALF // 2, HALF // 2)
    carry_out(0, recv_f.at[0], gi_buf.at[1], HALF // 2, HALF // 2)
    send_input_grad(0)
    finish_left(0)
    lr_copy = pltpu.make_async_remote_copy(
        src_ref=lr.at[other], dst_ref=lr_sib, send_sem=lr_send, recv_sem=lr_recv,
        device_id=sibling, device_id_type=MESH,
    )
    lr_copy.start()
    for number in range(3, 8):
        reduce_stage(0, number)
    swap_copy = pltpu.make_async_remote_copy(
        src_ref=gx.at[other], dst_ref=swap_buf, send_sem=swap_send, recv_sem=swap_recv,
        device_id=sibling, device_id_type=MESH,
    )
    swap_copy.start()
    chan_out[core] = gx[core].reshape(HR, T).astype(F32)
    lr_copy.wait()
    right_out[...] = lr[core, 0] + lr_sib[0]
    left_out[...] = lr[core, 1] + lr_sib[1]
    swap_copy.wait()
    chan_out[other] = swap_buf[...].reshape(HR, T).astype(F32)

    for copy in ex_copies:
        copy.wait_send()
    await_block(send_b.at[1], a2a_send, 0, 0, HALF)
    await_block(send_f.at[1], a2a_send, 1, 0, HALF)
    await_block(send_f.at[0], a2a_send, 2, 0, HALF // 2)
    await_block(send_b.at[0], a2a_send, 3, 0, HALF)
    await_block(send_f.at[0], a2a_send, 4, HALF // 2, HALF // 2)
    pltpu.make_async_copy(gi_buf.at[0], gi_out.at[0], gi_loc).wait()
    pltpu.make_async_copy(gi_buf.at[0], gi_out.at[0], gi_send).wait()
    pltpu.make_async_copy(gi_buf.at[0], gi_out.at[0], gi_recv).wait()


def body(x_saved, cotangent, seq_right, seq_left, chan_first, chan_second):
    v, dma = pltpu.VMEM, pltpu.SemaphoreType.DMA
    anywhere = pl.BlockSpec(memory_space=pl.ANY)
    vmem = pl.BlockSpec(memory_space=pltpu.VMEM)
    gi, right, left, chan = pl.pallas_call(
        kernel,
        name="monarch_backward",
        out_shape=[
            jax.ShapeDtypeStruct((2, T, D), BF16),
            jax.ShapeDtypeStruct((T, T), F32),
            jax.ShapeDtypeStruct((T, T), F32),
            jax.ShapeDtypeStruct((2, HR, T), F32),
        ],
        in_specs=[anywhere] * 6,
        out_specs=[anywhere, vmem, vmem, vmem],
        scratch_shapes=[
            v((2, T, D), BF16), v((2, T, T), BF16), v((2, T, T), BF16),
            v((2, D, NK), BF16), v((2, NK, NK, NK), BF16),
            v((T, D), BF16), v((2, T, D), BF16), v((2 * T, HALF), BF16), v((2, D, T), BF16),
            v((NK, NK, T), BF16), v((3, NK, NK, T), BF16), v((2, HALF, 2 * T), BF16),
            v((HALF, 2 * T), BF16), v((T, D), F32),
            v((2, 2 * T, 2 * T), BF16), v((2, 2 * T, 2 * T), BF16), v((2, 2 * T, 2 * T), BF16),
            v((2, 2 * T, HALF), BF16), v((2, 2 * T, HALF), BF16),
            v((2, 2 * T, HALF), BF16), v((2, 2 * T, HALF), BF16),
            v((5, 2, HALF), BF16), v((2 * T, 2 * T), F32), v((2 * T, T), F32),
            v((2, 2, HR, T), F32), v((2, HR, T), F32),
            v((2, HR, T), BF16), v((2, NX, HR // NX, T), BF16), v((2, HR // NX, T), F32),
            v((2, HR // NX, T), BF16), v((2, NY, T, T), BF16), v((3, T, T), F32),
            v((2, T, T), BF16), v((2, NZ, T // NZ, T), BF16),
            v((2, NZ, T // NZ, T), BF16), v((2, NY, T, T), BF16), v((2, NX, NY * T, T), BF16),
            v((NX, NY * T, T), BF16),
            v((2, 2, T, T), F32), v((2, T, T), F32),
            dma((2, 5)), dma((5,)), dma, dma((5,)), dma((5,)), dma((2, 27)), dma((2, 27)),
            dma, dma, dma, dma, dma, dma, dma, dma,
        ],
        compiler_params=pltpu.CompilerParams(
            collective_id=1, has_side_effects=True, vmem_limit_bytes=64_000_000
        ),
    )(
        x_saved[0], cotangent, seq_right[0, 0], seq_left[0, 0],
        chan_first[0].reshape(D, NK), chan_second[0],
    )

    def unpack(packed):
        return packed.reshape(NK // 2, NK, 2, NK).transpose(0, 2, 1, 3).reshape(1, NK, NK, NK)

    return (gi[None], right[None, None], left[None, None], unpack(chan[0]), unpack(chan[1]))


def solution(mesh):
    in_specs = (
        P("pipe", None, "blk", None),
        P(None, "blk", None),
        P("pipe", "blk", None, None),
        P("pipe", "blk", None, None),
        P("pipe", None, None, None),
        P("pipe", None, None, None),
    )
    out_specs = (
        P("pipe", None, "blk", None),
        P("pipe", "blk", None, None),
        P("pipe", "blk", None, None),
        P("pipe", None, None, None),
        P("pipe", None, None, None),
    )
    return jax.shard_map(body, mesh=mesh, in_specs=in_specs, out_specs=out_specs, check_vma=False)
```

time: 593 us -> 182 us (0.31); the launches traced: 582 us -> 179 us
  waiting for transfers between devices: 278 us -> 0 us
  Pallas kernels: 0 us -> 166 us
  local copies, waits for them, and re-layouts: 125 us -> 12.8 us
  matrix products: 74.1 us -> 0 us
  starting transfers between devices: 65 us -> 0 us
  other arithmetic: 24.8 us -> 0 us
  between operations: 14.8 us -> 0.67 us
    psum x1 -> x0, waiting for transfers between devices: 209 us -> none  [body(): first_total, second_total = lax.psum((first_acc, second_acc), 'blk')]
    pallas_call x0 -> x1, Pallas kernels: none -> 166 us  [body(): pl.pallas_call(kernel, name='monarch_backward', out_shape=[jax.ShapeDtype...]
    unnamed x121 -> x9, local copies, waits for them, and re-layouts: 94.1 us -> 3.32 us
    dot_general x36 -> x0, matrix products: 74.1 us -> none  [the longest x3 11.1 us: finish(): jnp.einsum('kms,kas->kma', hidden_grad, mixed_k, preferred_element_type=j...]
    all_to_all x6 -> x0, waiting for transfers between devices: 69.8 us -> none  [the longest x3 47.5 us: body(): lax.all_to_all(back_rows, 'blk', split_axis=0, concat_axis=1, tiled=True)]
    all_to_all x6 -> x0, starting transfers between devices: 61.8 us -> none  [the longest x3 38.1 us: body(): lax.all_to_all(back_rows, 'blk', split_axis=0, concat_axis=1, tiled=True)]
    convert_element_type x6 -> x0, other arithmetic: 18 us -> none  [the longest x3 9.32 us: after_rows(): back_rows = jnp.einsum('kmi,kmd->ikd', left_block, gate_grad, preferred_e...]
    dynamic_slice x7 -> x0, local copies, waits for them, and re-layouts: 16.6 us -> none  [the longest x4 9.34 us: body(): lax.dynamic_index_in_dim(grad_store, slot_index, 0, keepdims=False)]
  transfers between devices with their start and end apart: 9 -> 0, of which waited for: 6 -> 0; matrix products, arithmetic and copies ran while one was open for 25% -> 0% of each run, Pallas kernels for 0% -> 0%
where the time goes in v2:
time: 182 us; the launch traced here: 179 us
  Pallas kernels  166 us (91%)
  local copies, waits for them, and re-layouts  12.8 us (7%)
    pallas_call x1, Pallas kernels, body(): pl.pallas_call(kernel, name='monarch_backward', out_shape=[jax.ShapeDtype...  166 us
    another operation x2, local copies, waits for them, and re-layouts, unpack(): packed.reshape(NK // 2, NK, 2, NK).transpose(0, 2, 1, 3)  3.65 us

profile of v2, /device:TPU:32, one launch (start us, length us, event | category | flops | bytes accessed | tf_op | source)
XLA Modules:
  0.0 179.1 jit_solution(621098931582735194)
XLA Ops:
  0.6 165.6 %monarch_backward.1 = (bf16[2,128,4096]{2,1,0:T(8,128)(2,1)}, f32[128,128]{1,0:T(8,128)}, f32[128,128]{1,0:T(8,128)}, f32[2,2048,128]{2,1,0:T(8,128)}) custom-call(bf16[2,128,4096]{2,1,0:T(8,128)(2,1)} %bitcast.14, bf16[2,128,4096]{2,1,0:T(8,128)(2,1)} %cot_in.1, bf16[128,128]{1,0:T(8,128)(2,1)} %bitcast.22, bf16[128,128]{1,0:T(8,128)(2,1)} %bitcast.23, ...), custom_call_target="tpu_custom_call" | custom-call | tf_op jit(solution)/shard_map/monarch_backward/pallas_call | solution.py:478
  166.3 2.6 %fusion = (f32[1,2048,128]{2,1,0:T(8,128)}, f32[1,2048,128]{2,1,0:T(8,128)S(1)}) fusion(f32[2,2048,128]{2,1,0:T(8,128)} %get-tuple-element.12), kind=kLoop, calls=%fused_computation | loop fusion | bytes 4194304 | tf_op jit(solution)/shard_map/slice | solution.py:520
  168.9 2.5 %reshape_squeeze.11 = f32[32,64,2,64]{3,2,1,0:T(2,128)S(1)} reshape(f32[1,2048,128]{2,1,0:T(8,128)} %get-tuple-element.13) | data formatting | bytes 2097152 | tf_op jit(solution)/shard_map/reshape;squeeze | solution.py:518
  171.4 1.6 copy.12
  173.0 1.2 reshape_squeeze.10
  174.2 0.0 copy-start
  174.2 1.6 copy.11
  175.8 0.7 copy-done
  176.6 0.0 copy-start.2
  176.6 0.0 copy-start.1
  176.6 1.3 copy.16
  177.9 0.0 copy-done.2
  177.9 0.6 copy.17
  178.5 0.0 copy-done.1
  178.5 0.6 copy.18
Async XLA Ops:
  174.2 2.3 %copy-start = (bf16[2,128,4096]{2,1,0:T(8,128)(2,1)S(1)}, bf16[2,128,4096]{2,1,0:T(8,128)(2,1)}, u32[]{:S(2)}) copy-start(bf16[2,128,4096]{2,1,0:T(8,128)(2,1)} %get-tuple-element.9) | copy-start | bytes 6291460
  176.6 1.3 copy-start.2
  176.6 2.0 %copy-start.1 = (f32[128,128]{1,0:T(8,128)S(1)}, f32[128,128]{1,0:T(8,128)}, u32[]{:S(2)}) copy-start(f32[128,128]{1,0:T(8,128)} %get-tuple-element.11) | copy-start | bytes 196612

commit v3 on v2

--- a/solution.py
+++ b/solution.py
@@ -27,7 +27,7 @@
 
 def kernel(
     x_in, cot_in, right_in, left_in, first_in, second_in,
-    gi_out, right_out, left_out, chan_out,
+    gi_out, right_out, left_out, first_out, second_out,
     x_buf, right_buf, left_buf, first_buf, second_buf,
     gy_buf, gi_buf, gate_buf, pair_buf, mt_buf, mk_buf, ht_buf, hg_buf, cb_buf,
     rexp, lexp, lexp_t,
@@ -35,7 +35,7 @@
     grads, sib, stage1, land1, acc1, stage2, land2, acc2, stage3, land3, gz, gy2, gx, swap_buf,
     lr, lr_sib,
     in_sem, ex_sem, cot_sem, a2a_send, a2a_recv, red_send, red_recv,
-    gi_loc, gi_send, gi_recv, lr_send, lr_recv, swap_send, swap_recv, out_sem,
+    gi_loc, gi_send, gi_recv, lr_send, lr_recv, swap_send, swap_recv,
 ):
     me = lax.axis_index("blk")
     core = lax.axis_index("pipe")
@@ -61,26 +61,24 @@
 
     pl.semaphore_signal(barrier, inc=1, device_id=sibling, device_id_type=MESH)
     lax.fori_loop(1, NB, greet, 0)
-    pl.semaphore_wait(barrier, NB)
 
     remote = (
         (x_in.at[other], x_buf), (left_in, left_buf), (right_in, right_buf),
         (first_in, first_buf), (second_in, second_buf),
     )
-    ex_copies = []
-    for i, (src, dst) in enumerate(remote):
-        copy = pltpu.make_async_remote_copy(
+
+    def exchange_copy(i):
+        src, dst = remote[i]
+        return pltpu.make_async_remote_copy(
             src_ref=src, dst_ref=dst.at[core], send_sem=ex_sem.at[i], recv_sem=in_sem.at[core, i],
             device_id=sibling, device_id_type=MESH,
         )
-        copy.start()
-        ex_copies.append(copy)
 
     def await_input(section, i):
         ref = (x_buf, left_buf, right_buf, first_buf, second_buf)[i].at[section]
         pltpu.make_async_copy(ref, ref, in_sem.at[section, i]).wait()
 
-    def all_to_all(src, dst, ident, lo, size):
+    def all_to_all(src, dst, recv_id, send_id, lo, size, first=0, count=NB):
         columns = pl.ds(lo, size)
 
         def rows(i):
@@ -90,21 +88,22 @@
             peer = lax.rem(me + step, NB)
             pltpu.make_async_remote_copy(
                 src_ref=src.at[rows(peer), columns], dst_ref=dst.at[rows(me), columns],
-                send_sem=a2a_send.at[ident], recv_sem=a2a_recv.at[ident],
+                send_sem=a2a_send.at[send_id], recv_sem=a2a_recv.at[recv_id],
                 device_id={"blk": peer}, device_id_type=MESH,
             ).start()
             return carry
 
-        lax.fori_loop(1, NB, send, 0)
-        pltpu.make_async_copy(
-            src.at[rows(me), columns], dst.at[rows(me), columns], a2a_recv.at[ident]
-        ).start()
-        pltpu.make_async_copy(
-            src.at[rows(me), columns], dummy.at[ident, :, columns], a2a_send.at[ident]
-        ).start()
-
-    def await_block(ref, sem, ident, lo, size):
-        part = ref.at[:, pl.ds(lo, size)]
+        lax.fori_loop(max(first, 1), first + count, send, 0)
+        if first == 0:
+            pltpu.make_async_copy(
+                src.at[rows(me), columns], dst.at[rows(me), columns], a2a_recv.at[recv_id]
+            ).start()
+            pltpu.make_async_copy(
+                src.at[rows(me), columns], dummy.at[recv_id, :, columns], a2a_send.at[send_id]
+            ).start()
+
+    def await_block(ref, sem, ident, lo, size, rows=2 * T):
+        part = ref.at[pl.ds(0, rows), pl.ds(lo, size)]
         pltpu.make_async_copy(part, part, sem.at[ident]).wait()
 
     def expand(section):
@@ -141,22 +140,25 @@
 
         lax.fori_loop(0, NK // 2, step, 0, unroll=4)
 
-    def gate(section, grad_out, sent):
+    def gate(section, grad_out, sent, lo, size):
         def step(i, carry):
-            cs = aligned(i, TILE)
+            off = lo + i * TILE
+            cs = pl.ds(pl.multiple_of(off, TILE), TILE)
             for h in range(2):
-                wide = pl.ds(pl.multiple_of(i * TILE + h * HALF, TILE), TILE)
+                wide = pl.ds(pl.multiple_of(off + h * HALF, TILE), TILE)
                 value = grad_out[:, wide].astype(F32) * x_buf[section, :, wide].astype(F32)
                 gate_buf[h * T : (h + 1) * T, cs] = value.astype(BF16)
             sent[:, cs] = mm(lexp_t[section], gate_buf[:, cs]).astype(BF16)
             return carry
 
-        lax.fori_loop(0, HALF // TILE, step, 0)
-
-    def swap_blocks(src, dst):
+        lax.fori_loop(0, size // TILE, step, 0)
+
+    def swap_blocks(src, dst, lo, size):
+        ps = pl.ds(lo, size)
+
         def step(g, carry):
-            block = src[:, pl.ds(pl.multiple_of(g * 16, 16), 16), :]
-            dst[aligned(g, 16), :, :] = jnp.swapaxes(block, 0, 1)
+            qs = aligned(g, 16)
+            dst[qs, ps, :] = jnp.swapaxes(src[ps, qs, :], 0, 1)
             return carry
 
         lax.fori_loop(0, NK // 16, step, 0)
@@ -169,7 +171,7 @@
             return carry
 
         lax.fori_loop(0, NK // 2, mixed, 0, unroll=4)
-        swap_blocks(mt_buf, mk_buf.at[section])
+        swap_blocks(mt_buf, mk_buf.at[section], 0, NK)
 
         def hidden(k, carry):
             rows = aligned(k, NK)
@@ -193,8 +195,12 @@
         tmp[...] = jnp.where(even, acc[:, :T], acc[:, T:])
         target[...] = tmp[pl.ds(0, T, stride=2), :] + tmp[pl.ds(1, T, stride=2), :]
 
-    def channel_back(section, returned):
-        acc[...] = jnp.zeros_like(acc)
+    def channel_back(section, returned, part, parts):
+        if part == 0:
+            acc[...] = jnp.zeros_like(acc)
+        tiles = HALF // TILE // parts
+        pairs = NK // 4 // parts
+        first_half = lax.broadcasted_iota(jnp.int32, (NK, T), 1) < NK
 
         def step(i, carry):
             cs = aligned(i, TILE)
@@ -202,9 +208,7 @@
             hg_buf[cs, :] = mm(returned[:, cs], rexp[section], 0, 0).astype(BF16)
             return carry
 
-        lax.fori_loop(0, HALF // TILE, step, 0)
-        fold(lr.at[section, 0])
-        first_half = lax.broadcasted_iota(jnp.int32, (NK, T), 1) < NK
+        lax.fori_loop(part * tiles, (part + 1) * tiles, step, 0)
 
         def pair(b, carry):
             for h in range(2):
@@ -220,8 +224,12 @@
                     mt_buf[k0 + q] = back.astype(BF16)
             return carry
 
-        lax.fori_loop(0, NK // 4, pair, 0, unroll=2)
-        swap_blocks(mt_buf, mg_view)
+        lax.fori_loop(part * pairs, (part + 1) * pairs, pair, 0, unroll=2)
+        for h in range(2):
+            swap_blocks(mt_buf, mg_view, h * (NK // 2) + part * 2 * pairs, 2 * pairs)
+        if part < parts - 1:
+            return
+        fold(lr.at[section, 0])
 
         def columns(b, carry):
             cols = aligned(b, T)
@@ -256,17 +264,21 @@
 
     tmp2 = acc2.at[2]
 
-    def send_input_grad(section):
-        @pl.when(core == section)
-        def _():
-            pltpu.make_async_copy(gi_buf.at[section], gi_out.at[core], gi_loc).start()
-
-        @pl.when(core != section)
-        def _():
-            pltpu.make_async_remote_copy(
-                src_ref=gi_buf.at[section], dst_ref=gi_out.at[core], send_sem=gi_send, recv_sem=gi_recv,
-                device_id=sibling, device_id_type=MESH,
-            ).start()
+    def send_input_grad(section, lo, size):
+        for h in range(2):
+            cols = pl.ds(h * HALF + lo, size)
+            src, dst = gi_buf.at[section, :, cols], gi_out.at[core, :, cols]
+
+            @pl.when(core == section)
+            def _():
+                pltpu.make_async_copy(src, dst, gi_loc).start()
+
+            @pl.when(core != section)
+            def _():
+                pltpu.make_async_remote_copy(
+                    src_ref=src, dst_ref=dst, send_sem=gi_send, recv_sem=gi_recv,
+                    device_id=sibling, device_id_type=MESH,
+                ).start()
 
     is_low = core == 0
     coord1, coord2 = jnp.where(is_low, px, py), jnp.where(is_low, py, px)
@@ -389,83 +401,155 @@
         else:
             finish(g1())
 
+    def unpack(packed, out):
+        def step(b, carry):
+            block = packed(b).astype(F32)
+            out[2 * b] = block[:, :NK]
+            out[2 * b + 1] = block[:, NK:]
+            return carry
+
+        lax.fori_loop(0, NK // 2, step, 0, unroll=4)
+
+    for i in range(5):
+        await_input(core, i)
+    expand(core)
+    expand_right(core)
+    build_pairs(core)
     cot_copy.wait()
-    await_input(1, 1)
-    expand(1)
-    await_input(1, 0)
-    gate(1, gy_buf, send_b.at[1])
-    all_to_all(send_b.at[1], recv_b.at[1], 0, 0, HALF)
-
-    await_input(1, 2)
-    expand_right(1)
-    await_input(1, 3)
-    build_pairs(1)
-    await_input(1, 4)
+    pl.semaphore_wait(barrier, NB)
+    for i in (1, 0, 2, 3, 4):
+        exchange_copy(i).start()
+    await_input(other, 1)
+    expand(other)
+
+    @pl.when(core == 0)
+    def _():
+        await_input(1, 0)
+
+    gate(1, gy_buf, send_b.at[1], 0, HALF)
+    all_to_all(send_b.at[1], recv_b.at[1], 0, 0, 0, HALF)
+
+    for i in (2, 3, 4):
+        await_input(other, i)
+    expand_right(other)
+    build_pairs(other)
     forward(1, send_f.at[1])
-    all_to_all(send_f.at[1], recv_f.at[1], 1, 0, HALF)
-
-    for i in range(5):
-        await_input(0, i)
-    expand(0)
-    expand_right(0)
-    build_pairs(0)
+    PART = HALF // 2
+    for p in range(2):
+        all_to_all(send_f.at[1], recv_f.at[1], 1 + p, 1 + p, p * PART, PART)
+
+    @pl.when(core == 1)
+    def _():
+        await_input(0, 0)
+
     forward(0, send_f.at[0])
-    all_to_all(send_f.at[0], recv_f.at[0], 2, 0, HALF // 2)
 
     await_block(recv_b.at[1], a2a_recv, 0, 0, HALF)
-    channel_back(1, recv_b.at[1])
+    channel_back(1, recv_b.at[1], 0, 1)
     reduce_stage(1, 0)
     reduce_stage(1, 1)
 
-    await_block(recv_f.at[1], a2a_recv, 1, 0, HALF)
     acc[...] = jnp.zeros_like(acc)
-    carry_out(1, recv_f.at[1], gy_buf, 0, HALF)
+    for p in range(2):
+        await_block(recv_f.at[1], a2a_recv, 1 + p, p * PART, PART)
+        carry_out(1, recv_f.at[1], gy_buf, p * PART, PART)
+        gate(0, gi_buf.at[1], send_b.at[0], p * PART, PART)
+        if p == 1:
+            reduce_stage(1, 2)
+        all_to_all(send_b.at[0], recv_b.at[0], 3 + p, 3 + p, p * PART, PART)
+        send_input_grad(1, p * PART, PART)
     finish_left(1)
-    gate(0, gi_buf.at[1], send_b.at[0])
-    all_to_all(send_b.at[0], recv_b.at[0], 3, 0, HALF)
-    all_to_all(send_f.at[0], recv_f.at[0], 4, HALF // 2, HALF // 2)
-    send_input_grad(1)
-    for number in range(2, 8):
-        reduce_stage(1, number)
-
-    await_block(recv_b.at[0], a2a_recv, 3, 0, HALF)
-    channel_back(0, recv_b.at[0])
+
+    GROUP = 32
+    groups = [(p, g) for p in range(2) for g in range(NB // GROUP)]
+
+    def pump(n):
+        if n >= 2:
+            p, g = groups[n - 2]
+            await_block(send_f.at[0], a2a_send, 5 + n - 2, p * PART, PART, 2 * GROUP)
+        if n < len(groups):
+            p, g = groups[n]
+            all_to_all(send_f.at[0], recv_f.at[0], 5 + p, 5 + n, p * PART, PART, g * GROUP, GROUP)
+
+    await_block(recv_b.at[0], a2a_recv, 3, 0, PART)
+    channel_back(0, recv_b.at[0], 0, 2)
+    reduce_stage(1, 3)
+    pump(0)
+    pump(1)
+    await_block(recv_b.at[0], a2a_recv, 4, PART, PART)
+    channel_back(0, recv_b.at[0], 1, 2)
     reduce_stage(0, 0)
+    pump(2)
+    reduce_stage(1, 4)
     reduce_stage(0, 1)
-    await_block(recv_f.at[0], a2a_recv, 2, 0, HALF // 2)
+    pump(3)
+    reduce_stage(1, 5)
+    pump(4)
+    reduce_stage(0, 2)
+    reduce_stage(1, 6)
+    pump(5)
     acc[...] = jnp.zeros_like(acc)
-    carry_out(0, recv_f.at[0], gi_buf.at[1], 0, HALF // 2)
-    reduce_stage(0, 2)
-    await_block(recv_f.at[0], a2a_recv, 4, HALF // 2, HALF // 2)
-    carry_out(0, recv_f.at[0], gi_buf.at[1], HALF // 2, HALF // 2)
-    send_input_grad(0)
+    await_block(recv_f.at[0], a2a_recv, 5, 0, PART)
+    carry_out(0, recv_f.at[0], gi_buf.at[1], 0, PART)
+    send_input_grad(0, 0, PART)
+    reduce_stage(0, 3)
+    pump(6)
+    reduce_stage(1, 7)
+    reduce_stage(0, 4)
+    pump(7)
+    reduce_stage(0, 5)
+    await_block(recv_f.at[0], a2a_recv, 6, PART, PART)
+    carry_out(0, recv_f.at[0], gi_buf.at[1], PART, PART)
+    send_input_grad(0, PART, PART)
+    reduce_stage(0, 6)
     finish_left(0)
     lr_copy = pltpu.make_async_remote_copy(
         src_ref=lr.at[other], dst_ref=lr_sib, send_sem=lr_send, recv_sem=lr_recv,
         device_id=sibling, device_id_type=MESH,
     )
     lr_copy.start()
-    for number in range(3, 8):
-        reduce_stage(0, number)
+    reduce_stage(0, 7)
     swap_copy = pltpu.make_async_remote_copy(
         src_ref=gx.at[other], dst_ref=swap_buf, send_sem=swap_send, recv_sem=swap_recv,
         device_id=sibling, device_id_type=MESH,
     )
     swap_copy.start()
-    chan_out[core] = gx[core].reshape(HR, T).astype(F32)
+
+    def own_block(section):
+        return lambda b: gx[section, lax.div(b, 8), pl.ds(pl.multiple_of(lax.rem(b, 8) * NK, NK), NK), :]
+
+    def swap_block(b):
+        return swap_buf[lax.div(b, 8), pl.ds(pl.multiple_of(lax.rem(b, 8) * NK, NK), NK), :]
+
+    @pl.when(core == 0)
+    def _():
+        unpack(own_block(0), first_out)
+
+    @pl.when(core == 1)
+    def _():
+        unpack(own_block(1), second_out)
+
     lr_copy.wait()
     right_out[...] = lr[core, 0] + lr_sib[0]
     left_out[...] = lr[core, 1] + lr_sib[1]
     swap_copy.wait()
-    chan_out[other] = swap_buf[...].reshape(HR, T).astype(F32)
-
-    for copy in ex_copies:
-        copy.wait_send()
+
+    @pl.when(core == 0)
+    def _():
+        unpack(swap_block, second_out)
+
+    @pl.when(core == 1)
+    def _():
+        unpack(swap_block, first_out)
+
+    for i in range(5):
+        exchange_copy(i).wait_send()
     await_block(send_b.at[1], a2a_send, 0, 0, HALF)
-    await_block(send_f.at[1], a2a_send, 1, 0, HALF)
-    await_block(send_f.at[0], a2a_send, 2, 0, HALF // 2)
-    await_block(send_b.at[0], a2a_send, 3, 0, HALF)
-    await_block(send_f.at[0], a2a_send, 4, HALF // 2, HALF // 2)
+    for p in range(2):
+        await_block(send_f.at[1], a2a_send, 1 + p, p * PART, PART)
+        await_block(send_b.at[0], a2a_send, 3 + p, p * PART, PART)
+    pump(8)
+    pump(9)
     pltpu.make_async_copy(gi_buf.at[0], gi_out.at[0], gi_loc).wait()
     pltpu.make_async_copy(gi_buf.at[0], gi_out.at[0], gi_send).wait()
     pltpu.make_async_copy(gi_buf.at[0], gi_out.at[0], gi_recv).wait()
@@ -475,17 +559,18 @@
     v, dma = pltpu.VMEM, pltpu.SemaphoreType.DMA
     anywhere = pl.BlockSpec(memory_space=pl.ANY)
     vmem = pl.BlockSpec(memory_space=pltpu.VMEM)
-    gi, right, left, chan = pl.pallas_call(
+    gi, right, left, first, second = pl.pallas_call(
         kernel,
         name="monarch_backward",
         out_shape=[
             jax.ShapeDtypeStruct((2, T, D), BF16),
             jax.ShapeDtypeStruct((T, T), F32),
             jax.ShapeDtypeStruct((T, T), F32),
-            jax.ShapeDtypeStruct((2, HR, T), F32),
+            jax.ShapeDtypeStruct((NK, NK, NK), F32),
+            jax.ShapeDtypeStruct((NK, NK, NK), F32),
         ],
         in_specs=[anywhere] * 6,
-        out_specs=[anywhere, vmem, vmem, vmem],
+        out_specs=[anywhere, vmem, vmem, vmem, vmem],
         scratch_shapes=[
             v((2, T, D), BF16), v((2, T, T), BF16), v((2, T, T), BF16),
             v((2, D, NK), BF16), v((2, NK, NK, NK), BF16),
@@ -495,7 +580,7 @@
             v((2, 2 * T, 2 * T), BF16), v((2, 2 * T, 2 * T), BF16), v((2, 2 * T, 2 * T), BF16),
             v((2, 2 * T, HALF), BF16), v((2, 2 * T, HALF), BF16),
             v((2, 2 * T, HALF), BF16), v((2, 2 * T, HALF), BF16),
-            v((5, 2, HALF), BF16), v((2 * T, 2 * T), F32), v((2 * T, T), F32),
+            v((7, 2, HALF), BF16), v((2 * T, 2 * T), F32), v((2 * T, T), F32),
             v((2, 2, HR, T), F32), v((2, HR, T), F32),
             v((2, HR, T), BF16), v((2, NX, HR // NX, T), BF16), v((2, HR // NX, T), F32),
             v((2, HR // NX, T), BF16), v((2, NY, T, T), BF16), v((3, T, T), F32),
@@ -503,8 +588,8 @@
             v((2, NZ, T // NZ, T), BF16), v((2, NY, T, T), BF16), v((2, NX, NY * T, T), BF16),
             v((NX, NY * T, T), BF16),
             v((2, 2, T, T), F32), v((2, T, T), F32),
-            dma((2, 5)), dma((5,)), dma, dma((5,)), dma((5,)), dma((2, 27)), dma((2, 27)),
-            dma, dma, dma, dma, dma, dma, dma, dma,
+            dma((2, 5)), dma((5,)), dma, dma((13,)), dma((7,)), dma((2, 27)), dma((2, 27)),
+            dma, dma, dma, dma, dma, dma, dma,
         ],
         compiler_params=pltpu.CompilerParams(
             collective_id=1, has_side_effects=True, vmem_limit_bytes=64_000_000
@@ -514,10 +599,7 @@
         chan_first[0].reshape(D, NK), chan_second[0],
     )
 
-    def unpack(packed):
-        return packed.reshape(NK // 2, NK, 2, NK).transpose(0, 2, 1, 3).reshape(1, NK, NK, NK)
-
-    return (gi[None], right[None, None], left[None, None], unpack(chan[0]), unpack(chan[1]))
+    return (gi[None], right[None, None], left[None, None], first[None], second[None])
 
 
 def solution(mesh):

time: 182 us -> 146 us (0.80)
  Pallas kernels: 166 us -> 135 us
  local copies, waits for them, and re-layouts: 12.8 us -> 8.22 us
    pallas_call x1, Pallas kernels: 166 us -> 135 us  [body(): pl.pallas_call(kernel, name='monarch_backward', out_shape=[jax.ShapeDtype...]
    unnamed x9 -> x13, local copies, waits for them, and re-layouts: 3.32 us -> 8.22 us
    another operation x2 -> x0, local copies, waits for them, and re-layouts: 3.65 us -> none  [unpack(): packed.reshape(NK // 2, NK, 2, NK).transpose(0, 2, 1, 3)]
    transpose x2 -> x0, local copies, waits for them, and re-layouts: 3.21 us -> none  [unpack(): packed.reshape(NK // 2, NK, 2, NK).transpose(0, 2, 1, 3)]
    slice x1 -> x0, local copies, waits for them, and re-layouts: 2.65 us -> none  [body(): chan[1]]
where the time goes in v3:
time: 146 us; the launch traced here: 144 us
  Pallas kernels  135 us (92%)
  local copies, waits for them, and re-layouts  8.22 us (6%)
    pallas_call x1, Pallas kernels, body(): pl.pallas_call(kernel, name='monarch_backward', out_shape=[jax.ShapeDtype...  135 us
    unnamed x13, local copies, waits for them, and re-layouts  8.22 us

profile of v3, /device:TPU:32, one launch (start us, length us, event | category | flops | bytes accessed | tf_op | source)
XLA Modules:
  0.0 143.5 jit_solution(8435783837961782692)
XLA Ops:
  0.6 134.6 %monarch_backward.1 = (bf16[2,128,4096]{2,1,0:T(8,128)(2,1)}, f32[128,128]{1,0:T(8,128)}, f32[128,128]{1,0:T(8,128)}, f32[64,64,64]{2,1,0:T(8,128)}, f32[64,64,64]{2,1,0:T(8,128)}) custom-call(bf16[2,128,4096]{2,1,0:T(8,128)(2,1)} %bitcast.10, bf16[2,128,4096]{2,1,0:T(8,128)(2,1)} %cot_in.1, bf16[128,128]{1,0:T(8,128)(2,1)} %bitcast.18, ...), custom_call_target="tpu_custom_call" | custom-call | tf_op jit(solution)/shard_map/monarch_backward/pallas_call | solution.py:562
  135.3 0.0 copy-start.3
  135.3 0.0 copy-start.2
  135.3 0.0 copy-start.1
  135.3 3.3 %copy.16 = bf16[1,2,128,4096]{3,2,1,0:T(8,128)(2,1)} copy(bf16[1,2,128,4096]{3,2,1,0:T(8,128)(2,1)} %bitcast.13) | data formatting | bytes 4194304
  138.6 0.0 copy-done.3
  138.6 0.6 copy.17
  139.2 0.0 copy-done.2
  139.2 0.6 copy.18
  139.8 0.0 copy-done.1
  139.8 0.0 copy-start
  139.8 1.3 copy.19
  141.2 1.0 copy-done
  142.2 1.3 copy.20
Async XLA Ops:
  135.3 3.3 %copy-start.3 = (f32[128,128]{1,0:T(8,128)S(1)}, f32[128,128]{1,0:T(8,128)}, u32[]{:S(2)}) copy-start(f32[128,128]{1,0:T(8,128)} %get-tuple-element.11) | copy-start | bytes 196612
  135.3 3.9 %copy-start.2 = (f32[128,128]{1,0:T(8,128)S(1)}, f32[128,128]{1,0:T(8,128)}, u32[]{:S(2)}) copy-start(f32[128,128]{1,0:T(8,128)} %get-tuple-element.12) | copy-start | bytes 196612
  135.3 4.6 %copy-start.1 = (f32[64,64,64]{2,1,0:T(8,128)S(1)}, f32[64,64,64]{2,1,0:T(8,128)}, u32[]{:S(2)}) copy-start(f32[64,64,64]{2,1,0:T(8,128)} %get-tuple-element.13) | copy-start | bytes 3145732
  139.8 2.3 %copy-start = (f32[64,64,64]{2,1,0:T(8,128)S(1)}, f32[64,64,64]{2,1,0:T(8,128)}, u32[]{:S(2)}) copy-start(f32[64,64,64]{2,1,0:T(8,128)} %get-tuple-element.14) | copy-start | bytes 3145732

commit v4 on v3

--- a/solution.py
+++ b/solution.py
@@ -32,10 +32,9 @@
     gy_buf, gi_buf, gate_buf, pair_buf, mt_buf, mk_buf, ht_buf, hg_buf, cb_buf,
     rexp, lexp, lexp_t,
     send_f, recv_f, send_b, recv_b, dummy, acc, tmp,
-    grads, sib, stage1, land1, acc1, stage2, land2, acc2, stage3, land3, gz, gy2, gx, swap_buf,
-    lr, lr_sib,
+    grads, stage0, sib, stage1, land1, acc1, stage2, land2, total, gx, lr, lr_sib, left_sum,
     in_sem, ex_sem, cot_sem, a2a_send, a2a_recv, red_send, red_recv,
-    gi_loc, gi_send, gi_recv, lr_send, lr_recv, swap_send, swap_recv,
+    gi_loc, gi_send, gi_recv, lr_send, lr_recv,
 ):
     me = lax.axis_index("blk")
     core = lax.axis_index("pipe")
@@ -61,6 +60,14 @@
 
     pl.semaphore_signal(barrier, inc=1, device_id=sibling, device_id_type=MESH)
     lax.fori_loop(1, NB, greet, 0)
+    for d in range(1, NX):
+        for axis_peer in (
+            me + (lax.rem(px + d, NX) - px) * (NZ * NY),
+            me + (lax.rem(py + d, NY) - py),
+        ):
+            pl.semaphore_signal(
+                barrier, inc=1, device_id={"blk": axis_peer, "pipe": other}, device_id_type=MESH
+            )
 
     remote = (
         (x_in.at[other], x_buf), (left_in, left_buf), (right_in, right_buf),
@@ -195,16 +202,24 @@
         tmp[...] = jnp.where(even, acc[:, :T], acc[:, T:])
         target[...] = tmp[pl.ds(0, T, stride=2), :] + tmp[pl.ds(1, T, stride=2), :]
 
-    def channel_back(section, returned, part, parts):
-        if part == 0:
-            acc[...] = jnp.zeros_like(acc)
+    def right_back(section, returned):
+        acc[...] = jnp.zeros_like(acc)
+
+        def step(i, carry):
+            cs = aligned(i, TILE)
+            acc[...] += mm(returned[:, cs], ht_buf[section, cs, :])
+            return carry
+
+        lax.fori_loop(0, HALF // TILE, step, 0)
+        fold(lr.at[section, 0])
+
+    def channel_back(section, returned, part, parts, between=lambda: None):
         tiles = HALF // TILE // parts
         pairs = NK // 4 // parts
         first_half = lax.broadcasted_iota(jnp.int32, (NK, T), 1) < NK
 
         def step(i, carry):
             cs = aligned(i, TILE)
-            acc[...] += mm(returned[:, cs], ht_buf[section, cs, :])
             hg_buf[cs, :] = mm(returned[:, cs], rexp[section], 0, 0).astype(BF16)
             return carry
 
@@ -229,13 +244,21 @@
             swap_blocks(mt_buf, mg_view, h * (NK // 2) + part * 2 * pairs, 2 * pairs)
         if part < parts - 1:
             return
-        fold(lr.at[section, 0])
+        between()
 
         def columns(b, carry):
             cols = aligned(b, T)
             mixed_grad = mg_view[aligned(b, 2)].reshape(T, T)
             outer = mm(mixed_grad, x_buf[section, :, cols])
             grads[section, 0, aligned(b, NK), :] = jnp.where(first_half, outer[:NK], outer[NK:])
+            return carry
+
+        lax.fori_loop(0, NK // 2, columns, 0, unroll=4)
+
+    def channel_out(section):
+        def columns(b, carry):
+            cols = aligned(b, T)
+            mixed_grad = mg_view[aligned(b, 2)].reshape(T, T)
             cb_buf[:, cols] = mm(mixed_grad, pair_buf[section, cols, :], 0, 0)
             return carry
 
@@ -259,10 +282,8 @@
         lax.fori_loop(0, size // TILE, step, 0)
 
     def finish_left(section):
-        fold(tmp2)
-        lr[section, 1] = tmp2[...].T
-
-    tmp2 = acc2.at[2]
+        fold(left_sum)
+        lr[section, 1] = left_sum[...].T
 
     def send_input_grad(section, lo, size):
         for h in range(2):
@@ -283,127 +304,133 @@
     is_low = core == 0
     coord1, coord2 = jnp.where(is_low, px, py), jnp.where(is_low, py, px)
     stride1, stride2 = jnp.where(is_low, NZ * NY, 1), jnp.where(is_low, 1, NZ * NY)
-    axes = ((coord1, stride1, NX), (coord2, stride2, NY), (pz, NY, NZ))
-
-    def hop(axis, d):
-        coord, stride, size = axes[axis]
-        return {"blk": me + (lax.rem(coord + d, size) - coord) * stride}
-
-    def copies(section, base, axis, src_of, dst_of):
-        size = axes[axis][2]
-        return [
-            pltpu.make_async_remote_copy(
-                src_ref=src_of(d), dst_ref=dst_of(d),
-                send_sem=red_send.at[section, base + d], recv_sem=red_recv.at[section, base + d],
-                device_id=hop(axis, d), device_id_type=MESH,
-            )
-            for d in range(1, size)
-        ]
-
-    def scatter(section, base, axis, stage, landing):
-        coord, _, size = axes[axis]
-        rows = landing.shape[2]
-        return copies(
-            section, base, axis,
-            lambda d: stage.at[section, aligned(lax.rem(coord + d, size), rows)],
-            lambda d: landing.at[section, d],
-        )
-
-    def gather(section, base, axis, buf):
-        coord = axes[axis][0]
-        return copies(
-            section, base, axis,
-            lambda d: buf.at[section, coord],
-            lambda d: buf.at[section, coord],
-        )
-
-    def sib_copy(section):
+    PIECE = HR // NX
+    PLANE = NY * NZ
+    SUB = PIECE // PLANE
+
+    def hop(d):
+        return me + (lax.rem(coord1 + d, NX) - coord1) * stride1
+
+    def sib_copy(section, d):
         return pltpu.make_async_remote_copy(
-            src_ref=grads.at[section, other], dst_ref=sib.at[section],
-            send_sem=red_send.at[section, 0], recv_sem=red_recv.at[section, 0],
+            src_ref=stage0.at[section, d], dst_ref=sib.at[section, d],
+            send_sem=red_send.at[section, d], recv_sem=red_recv.at[section, d],
             device_id=sibling, device_id_type=MESH,
         )
 
-    def start(group):
-        for c in group:
-            c.start()
-
-    def finish(group):
-        for c in group:
-            c.wait()
-
-    def reduce_stage(section, number):
-        def s1():
-            return scatter(section, 0, 0, stage1, land1)
-
-        def s2():
-            return scatter(section, 3, 1, stage2, land2)
-
-        def s3():
-            return scatter(section, 6, 2, stage3, land3)
-
-        def g3():
-            return gather(section, 13, 2, gz)
-
-        def g2():
-            return gather(section, 20, 1, gy2)
-
-        def g1():
-            return gather(section, 23, 0, gx)
-
-        def settle(values, coord, landing, size):
-            rows = landing.shape[2]
-            total = values[aligned(coord, rows), :]
-            for d in range(1, size):
-                total = total + landing[section, d].astype(F32)
-            return total
-
-        if number == 0:
-            sib_copy(section).start()
-        elif number == 1:
-            sib_copy(section).wait()
-            mine = grads.at[section, core]
-
-            def add(i, carry):
-                rows = aligned(i, 256)
-                total = mine[rows, :] + sib[section, rows, :]
-                sib[section, rows, :] = total
-                stage1[section, rows, :] = total.astype(BF16)
-                return carry
-
-            lax.fori_loop(0, HR // 256, add, 0)
-            start(s1())
-        elif number == 2:
-            finish(s1())
-            value = settle(sib.at[section], coord1, land1, NX)
-            acc1[section] = value
-            stage2[section] = value.astype(BF16)
-            start(s2())
-        elif number == 3:
-            finish(s2())
-            value = settle(acc1.at[section], coord2, land2, NY)
-            acc2[section] = value
-            stage3[section] = value.astype(BF16)
-            start(s3())
-        elif number == 4:
-            finish(s3())
-            value = settle(acc2.at[section], pz, land3, NZ)
-            gz[section, pz] = value.astype(BF16)
-            start(g3())
-        elif number == 5:
-            finish(g3())
-            gy2[section, coord2] = gz[section].reshape(T, T)
-            start(g2())
-        elif number == 6:
-            finish(g2())
-            gx[section, coord1] = gy2[section].reshape(NY * T, T)
-            start(g1())
-        else:
-            finish(g1())
-
-    def unpack(packed, out):
+    def first_copy(section, d):
+        return pltpu.make_async_remote_copy(
+            src_ref=stage1.at[section, d], dst_ref=land1.at[section, d],
+            send_sem=red_send.at[section, 4 + d], recv_sem=red_recv.at[section, 4 + d],
+            device_id={"blk": hop(d)}, device_id_type=MESH,
+        )
+
+    def plane(u):
+        return lax.rem(coord2 + lax.div(u, NZ), NY), lax.rem(pz + lax.rem(u, NZ), NZ)
+
+    def plane_copy(section, u, src, dst, sem):
+        c2, cz = plane(u)
+        peer = me + (c2 - coord2) * stride2 + (cz - pz) * NY
+        return pltpu.make_async_remote_copy(
+            src_ref=src, dst_ref=dst, send_sem=red_send.at[section, sem], recv_sem=red_recv.at[section, sem],
+            device_id={"blk": peer}, device_id_type=MESH,
+        )
+
+    def await_plane(ref, section, sem):
+        part = ref.at[section, pl.ds(0, PLANE - 1)]
+        pltpu.make_async_copy(part, part, red_send.at[section, sem]).wait()
+        pltpu.make_async_copy(part, part, red_recv.at[section, sem]).wait()
+
+    def last_copy(section, d):
+        return pltpu.make_async_remote_copy(
+            src_ref=total.at[section], dst_ref=gx.at[core, coord1],
+            send_sem=red_send.at[section, 10 + d], recv_sem=red_recv.at[section, 10 + NX * core + d],
+            device_id={"blk": hop(d), "pipe": section}, device_id_type=MESH,
+        )
+
+    def reduce_siblings(section):
+        for d in (1, 2, 3, 0):
+            rows = aligned(lax.rem(coord2 + d, NX), PIECE)
+            stage0[section, d] = grads[section, other, rows, :].astype(BF16)
+            sib_copy(section, d).start()
+
+    def reduce_first(section):
+        for d in (1, 2, 3, 0):
+            rows = aligned(lax.rem(coord1 + d, NX), PIECE)
+            sib_copy(section, d).wait()
+            value = grads[section, core, rows, :] + sib[section, d].astype(F32)
+            if d:
+                stage1[section, d] = value.astype(BF16)
+                first_copy(section, d).start()
+            else:
+                acc1[section] = value
+
+    def reduce_plane(section):
+        for d in range(1, NX):
+            first_copy(section, d).wait()
+        value = acc1[section]
+        for d in range(1, NX):
+            value = value + land1[section, d].astype(F32)
+        acc1[section] = value
+        stage2[section] = value.astype(BF16).reshape(PLANE, SUB, T)
+
+        def send(u, carry):
+            c2, cz = plane(u)
+            plane_copy(section, u, stage2.at[section, c2 * NZ + cz], land2.at[section, u - 1], 8).start()
+            return carry
+
+        lax.fori_loop(1, PLANE, send, 0)
+
+    def gather_plane(section):
+        mine = coord2 * NZ + pz
+        await_plane(land2, section, 8)
+
+        def add(u, value):
+            return value + land2[section, u].astype(F32)
+
+        value = lax.fori_loop(0, PLANE - 1, add, acc1[section, aligned(mine, SUB), :], unroll=True)
+        total[section, mine] = value.astype(BF16)
+
+        def send(u, carry):
+            plane_copy(section, u, total.at[section, mine], total.at[section, mine], 9).start()
+            return carry
+
+        lax.fori_loop(1, PLANE, send, 0)
+
+    def gather_last(section):
+        await_plane(total, section, 9)
+        for d in range(1, NX):
+            last_copy(section, d).start()
+
+        @pl.when(core == section)
+        def _():
+            pltpu.make_async_copy(
+                total.at[section], gx.at[core, coord1], red_recv.at[section, 10 + NX * core]
+            ).start()
+
+        @pl.when(core != section)
+        def _():
+            last_copy(section, 0).start()
+
+    def await_last():
+        for h in range(2):
+            for d in range(NX):
+                part = gx.at[h, d]
+                pltpu.make_async_copy(part, part, red_recv.at[core, 10 + NX * h + d]).wait()
+
+    def await_last_sends():
+        for section in range(2):
+            for d in range(1, NX):
+                last_copy(section, d).wait_send()
+
+            @pl.when(core != section)
+            def _():
+                last_copy(section, 0).wait_send()
+
+    def unpack(half, out):
         def step(b, carry):
-            block = packed(b).astype(F32)
+            rows = aligned(lax.rem(b, 8), 4)
+            block = gx[half, lax.div(b, 8), rows].reshape(NK, T).astype(F32)
             out[2 * b] = block[:, :NK]
             out[2 * b + 1] = block[:, NK:]
             return carry
@@ -416,7 +443,7 @@
     expand_right(core)
     build_pairs(core)
     cot_copy.wait()
-    pl.semaphore_wait(barrier, NB)
+    pl.semaphore_wait(barrier, NB + NX + NY - 2)
     for i in (1, 0, 2, 3, 4):
         exchange_copy(i).start()
     await_input(other, 1)
@@ -446,8 +473,10 @@
 
     await_block(recv_b.at[1], a2a_recv, 0, 0, HALF)
     channel_back(1, recv_b.at[1], 0, 1)
-    reduce_stage(1, 0)
-    reduce_stage(1, 1)
+    reduce_siblings(1)
+    channel_out(1)
+    reduce_first(1)
+    right_back(1, recv_b.at[1])
 
     acc[...] = jnp.zeros_like(acc)
     for p in range(2):
@@ -455,7 +484,7 @@
         carry_out(1, recv_f.at[1], gy_buf, p * PART, PART)
         gate(0, gi_buf.at[1], send_b.at[0], p * PART, PART)
         if p == 1:
-            reduce_stage(1, 2)
+            reduce_plane(1)
         all_to_all(send_b.at[0], recv_b.at[0], 3 + p, 3 + p, p * PART, PART)
         send_input_grad(1, p * PART, PART)
     finish_left(1)
@@ -473,74 +502,49 @@
 
     await_block(recv_b.at[0], a2a_recv, 3, 0, PART)
     channel_back(0, recv_b.at[0], 0, 2)
-    reduce_stage(1, 3)
+    gather_plane(1)
     pump(0)
     pump(1)
     await_block(recv_b.at[0], a2a_recv, 4, PART, PART)
-    channel_back(0, recv_b.at[0], 1, 2)
-    reduce_stage(0, 0)
-    pump(2)
-    reduce_stage(1, 4)
-    reduce_stage(0, 1)
+
+
+    def between():
+        gather_last(1)
+        pump(2)
+
+    channel_back(0, recv_b.at[0], 1, 2, between)
+    reduce_siblings(0)
+    channel_out(0)
+    reduce_first(0)
     pump(3)
-    reduce_stage(1, 5)
+    right_back(0, recv_b.at[0])
+    reduce_plane(0)
     pump(4)
-    reduce_stage(0, 2)
-    reduce_stage(1, 6)
     pump(5)
+    gather_plane(0)
+    pump(6)
+    pump(7)
     acc[...] = jnp.zeros_like(acc)
     await_block(recv_f.at[0], a2a_recv, 5, 0, PART)
     carry_out(0, recv_f.at[0], gi_buf.at[1], 0, PART)
     send_input_grad(0, 0, PART)
-    reduce_stage(0, 3)
-    pump(6)
-    reduce_stage(1, 7)
-    reduce_stage(0, 4)
-    pump(7)
-    reduce_stage(0, 5)
+    gather_last(0)
     await_block(recv_f.at[0], a2a_recv, 6, PART, PART)
     carry_out(0, recv_f.at[0], gi_buf.at[1], PART, PART)
     send_input_grad(0, PART, PART)
-    reduce_stage(0, 6)
     finish_left(0)
     lr_copy = pltpu.make_async_remote_copy(
         src_ref=lr.at[other], dst_ref=lr_sib, send_sem=lr_send, recv_sem=lr_recv,
         device_id=sibling, device_id_type=MESH,
     )
     lr_copy.start()
-    reduce_stage(0, 7)
-    swap_copy = pltpu.make_async_remote_copy(
-        src_ref=gx.at[other], dst_ref=swap_buf, send_sem=swap_send, recv_sem=swap_recv,
-        device_id=sibling, device_id_type=MESH,
-    )
-    swap_copy.start()
-
-    def own_block(section):
-        return lambda b: gx[section, lax.div(b, 8), pl.ds(pl.multiple_of(lax.rem(b, 8) * NK, NK), NK), :]
-
-    def swap_block(b):
-        return swap_buf[lax.div(b, 8), pl.ds(pl.multiple_of(lax.rem(b, 8) * NK, NK), NK), :]
-
-    @pl.when(core == 0)
-    def _():
-        unpack(own_block(0), first_out)
-
-    @pl.when(core == 1)
-    def _():
-        unpack(own_block(1), second_out)
-
+    await_last()
+    unpack(0, first_out)
+    unpack(1, second_out)
     lr_copy.wait()
     right_out[...] = lr[core, 0] + lr_sib[0]
     left_out[...] = lr[core, 1] + lr_sib[1]
-    swap_copy.wait()
-
-    @pl.when(core == 0)
-    def _():
-        unpack(swap_block, second_out)
-
-    @pl.when(core == 1)
-    def _():
-        unpack(swap_block, first_out)
+    await_last_sends()
 
     for i in range(5):
         exchange_copy(i).wait_send()
@@ -570,7 +574,7 @@
             jax.ShapeDtypeStruct((NK, NK, NK), F32),
         ],
         in_specs=[anywhere] * 6,
-        out_specs=[anywhere, vmem, vmem, vmem, vmem],
+        out_specs=[vmem] * 5,
         scratch_shapes=[
             v((2, T, D), BF16), v((2, T, T), BF16), v((2, T, T), BF16),
             v((2, D, NK), BF16), v((2, NK, NK, NK), BF16),
@@ -581,15 +585,13 @@
             v((2, 2 * T, HALF), BF16), v((2, 2 * T, HALF), BF16),
             v((2, 2 * T, HALF), BF16), v((2, 2 * T, HALF), BF16),
             v((7, 2, HALF), BF16), v((2 * T, 2 * T), F32), v((2 * T, T), F32),
-            v((2, 2, HR, T), F32), v((2, HR, T), F32),
-            v((2, HR, T), BF16), v((2, NX, HR // NX, T), BF16), v((2, HR // NX, T), F32),
-            v((2, HR // NX, T), BF16), v((2, NY, T, T), BF16), v((3, T, T), F32),
-            v((2, T, T), BF16), v((2, NZ, T // NZ, T), BF16),
-            v((2, NZ, T // NZ, T), BF16), v((2, NY, T, T), BF16), v((2, NX, NY * T, T), BF16),
-            v((NX, NY * T, T), BF16),
-            v((2, 2, T, T), F32), v((2, T, T), F32),
-            dma((2, 5)), dma((5,)), dma, dma((13,)), dma((7,)), dma((2, 27)), dma((2, 27)),
-            dma, dma, dma, dma, dma, dma, dma,
+            v((2, 2, HR, T), F32), v((2, NX, HR // NX, T), BF16), v((2, NX, HR // NX, T), BF16),
+            v((2, NX, HR // NX, T), BF16), v((2, NX, HR // NX, T), BF16), v((2, HR // NX, T), F32),
+            v((2, NY * NZ, HR // NB, T), BF16), v((2, NY * NZ, HR // NB, T), BF16),
+            v((2, NY * NZ, HR // NB, T), BF16), v((2, NX, NY * NZ, HR // NB, T), BF16),
+            v((2, 2, T, T), F32), v((2, T, T), F32), v((T, T), F32),
+            dma((2, 5)), dma((5,)), dma, dma((13,)), dma((7,)), dma((2, 18)), dma((2, 18)),
+            dma, dma, dma, dma, dma,
         ],
         compiler_params=pltpu.CompilerParams(
             collective_id=1, has_side_effects=True, vmem_limit_bytes=64_000_000

time: 146 us -> 143 us (0.979); the launches traced: 144 us -> 143 us
  no operation moved by 1% of the time
where the time goes in v4:
time: 143 us
  Pallas kernels  134 us (94%)
  local copies, waits for them, and re-layouts  8.22 us (6%)
    pallas_call x1, Pallas kernels, body(): pl.pallas_call(kernel, name='monarch_backward', out_shape=[jax.ShapeDtype...  134 us
    unnamed x13, local copies, waits for them, and re-layouts  8.22 us

profile of v4, /device:TPU:32, one launch (start us, length us, event | category | flops | bytes accessed | tf_op | source)
XLA Modules:
  0.0 142.9 jit_solution(4793945893823739889)
XLA Ops:
  0.6 134.0 %monarch_backward.1 = (bf16[2,128,4096]{2,1,0:T(8,128)(2,1)}, f32[128,128]{1,0:T(8,128)}, f32[128,128]{1,0:T(8,128)}, f32[64,64,64]{2,1,0:T(8,128)}, f32[64,64,64]{2,1,0:T(8,128)}) custom-call(bf16[2,128,4096]{2,1,0:T(8,128)(2,1)} %bitcast.10, bf16[2,128,4096]{2,1,0:T(8,128)(2,1)} %cot_in.1, bf16[128,128]{1,0:T(8,128)(2,1)} %bitcast.18, ...), custom_call_target="tpu_custom_call" | custom-call | tf_op jit(solution)/shard_map/monarch_backward/pallas_call | solution.py:566
  134.7 0.0 copy-start.3
  134.7 0.0 copy-start.2
  134.7 0.0 copy-start.1
  134.7 3.3 %copy.16 = bf16[1,2,128,4096]{3,2,1,0:T(8,128)(2,1)} copy(bf16[1,2,128,4096]{3,2,1,0:T(8,128)(2,1)} %bitcast.13) | data formatting | bytes 4194304
  138.0 0.0 copy-done.3
  138.0 0.6 copy.17
  138.6 0.0 copy-done.2
  138.6 0.6 copy.18
  139.2 0.0 copy-done.1
  139.2 0.0 copy-start
  139.2 1.3 copy.19
  140.6 1.0 copy-done
  141.6 1.3 copy.20
Async XLA Ops:
  134.7 3.3 %copy-start.3 = (f32[128,128]{1,0:T(8,128)S(1)}, f32[128,128]{1,0:T(8,128)}, u32[]{:S(2)}) copy-start(f32[128,128]{1,0:T(8,128)} %get-tuple-element.11) | copy-start | bytes 196612
  134.7 3.9 %copy-start.2 = (f32[128,128]{1,0:T(8,128)S(1)}, f32[128,128]{1,0:T(8,128)}, u32[]{:S(2)}) copy-start(f32[128,128]{1,0:T(8,128)} %get-tuple-element.12) | copy-start | bytes 196612
  134.7 4.6 %copy-start.1 = (f32[64,64,64]{2,1,0:T(8,128)S(1)}, f32[64,64,64]{2,1,0:T(8,128)}, u32[]{:S(2)}) copy-start(f32[64,64,64]{2,1,0:T(8,128)} %get-tuple-element.13) | copy-start | bytes 3145732
  139.2 2.3 %copy-start = (f32[64,64,64]{2,1,0:T(8,128)S(1)}, f32[64,64,64]{2,1,0:T(8,128)}, u32[]{:S(2)}) copy-start(f32[64,64,64]{2,1,0:T(8,128)} %get-tuple-element.14) | copy-start | bytes 3145732

commit v5 on v4

--- a/solution.py
+++ b/solution.py
@@ -27,7 +27,7 @@
 
 def kernel(
     x_in, cot_in, right_in, left_in, first_in, second_in,
-    gi_out, right_out, left_out, first_out, second_out,
+    gi_own, gi_sib, right_out, left_out, first_out, second_out,
     x_buf, right_buf, left_buf, first_buf, second_buf,
     gy_buf, gi_buf, gate_buf, pair_buf, mt_buf, mk_buf, ht_buf, hg_buf, cb_buf,
     rexp, lexp, lexp_t,
@@ -85,7 +85,7 @@
         ref = (x_buf, left_buf, right_buf, first_buf, second_buf)[i].at[section]
         pltpu.make_async_copy(ref, ref, in_sem.at[section, i]).wait()
 
-    def all_to_all(src, dst, recv_id, send_id, lo, size, first=0, count=NB):
+    def all_to_all(src, dst, recv_id, send_id, lo, size, first=0, count=NB, extra=None):
         columns = pl.ds(lo, size)
 
         def rows(i):
@@ -98,10 +98,14 @@
                 send_sem=a2a_send.at[send_id], recv_sem=a2a_recv.at[recv_id],
                 device_id={"blk": peer}, device_id_type=MESH,
             ).start()
+            if extra is not None:
+                extra(step - first)
             return carry
 
         lax.fori_loop(max(first, 1), first + count, send, 0)
         if first == 0:
+            if extra is not None:
+                extra(jnp.int32(0))
             pltpu.make_async_copy(
                 src.at[rows(me), columns], dst.at[rows(me), columns], a2a_recv.at[recv_id]
             ).start()
@@ -288,22 +292,23 @@
     def send_input_grad(section, lo, size):
         for h in range(2):
             cols = pl.ds(h * HALF + lo, size)
-            src, dst = gi_buf.at[section, :, cols], gi_out.at[core, :, cols]
+            src = gi_buf.at[section, :, cols]
 
             @pl.when(core == section)
             def _():
-                pltpu.make_async_copy(src, dst, gi_loc).start()
+                pltpu.make_async_copy(src, gi_own.at[:, cols], gi_loc).start()
 
             @pl.when(core != section)
             def _():
                 pltpu.make_async_remote_copy(
-                    src_ref=src, dst_ref=dst, send_sem=gi_send, recv_sem=gi_recv,
+                    src_ref=src, dst_ref=gi_sib.at[:, cols], send_sem=gi_send, recv_sem=gi_recv,
                     device_id=sibling, device_id_type=MESH,
                 ).start()
 
     is_low = core == 0
     coord1, coord2 = jnp.where(is_low, px, py), jnp.where(is_low, py, px)
     stride1, stride2 = jnp.where(is_low, NZ * NY, 1), jnp.where(is_low, 1, NZ * NY)
+    GROUP = 32
     PIECE = HR // NX
     PLANE = NY * NZ
     SUB = PIECE // PLANE
@@ -361,9 +366,42 @@
             value = grads[section, core, rows, :] + sib[section, d].astype(F32)
             if d:
                 stage1[section, d] = value.astype(BF16)
-                first_copy(section, d).start()
             else:
                 acc1[section] = value
+
+    def first_piece(section, d, r):
+        rows = aligned(r, 16)
+        pltpu.make_async_remote_copy(
+            src_ref=stage1.at[section, d, rows], dst_ref=land1.at[section, d, rows],
+            send_sem=red_send.at[section, 4 + d], recv_sem=red_recv.at[section, 4 + d],
+            device_id={"blk": hop(d)}, device_id_type=MESH,
+        ).start()
+
+    def first_spread(step):
+        @pl.when((step >= 1) & (step <= 3 * (PIECE // 16)))
+        def _():
+            index = step - 1
+            first_piece(1, 1 + lax.rem(index, 3), lax.div(index, 3))
+
+    def first_burst(step):
+        for d in range(1, NX):
+            first_piece(0, d, step)
+
+    def last_piece(section, d, u, rows):
+        pltpu.make_async_remote_copy(
+            src_ref=total.at[section, u, rows], dst_ref=gx.at[core, coord1, u, rows],
+            send_sem=red_send.at[section, 10 + d], recv_sem=red_recv.at[section, 10 + NX * core + d],
+            device_id={"blk": hop(d), "pipe": section}, device_id_type=MESH,
+        ).start()
+
+    def last_burst(part):
+        def extra(step):
+            index = step + part * GROUP
+            rows = aligned(lax.rem(index, 2), SUB // 2)
+            for d in range(1, NX):
+                last_piece(1, d, lax.div(index, 2), rows)
+
+        return extra
 
     def reduce_plane(section):
         for d in range(1, NX):
@@ -397,10 +435,11 @@
 
         lax.fori_loop(1, PLANE, send, 0)
 
-    def gather_last(section):
+    def gather_last(section, pieces=False):
         await_plane(total, section, 9)
-        for d in range(1, NX):
-            last_copy(section, d).start()
+        if not pieces:
+            for d in range(1, NX):
+                last_copy(section, d).start()
 
         @pl.when(core == section)
         def _():
@@ -430,7 +469,7 @@
     def unpack(half, out):
         def step(b, carry):
             rows = aligned(lax.rem(b, 8), 4)
-            block = gx[half, lax.div(b, 8), rows].reshape(NK, T).astype(F32)
+            block = gx[half, lax.div(b, 8), rows].reshape(NK, T)
             out[2 * b] = block[:, :NK]
             out[2 * b + 1] = block[:, NK:]
             return carry
@@ -483,44 +522,40 @@
         await_block(recv_f.at[1], a2a_recv, 1 + p, p * PART, PART)
         carry_out(1, recv_f.at[1], gy_buf, p * PART, PART)
         gate(0, gi_buf.at[1], send_b.at[0], p * PART, PART)
-        if p == 1:
-            reduce_plane(1)
-        all_to_all(send_b.at[0], recv_b.at[0], 3 + p, 3 + p, p * PART, PART)
+        all_to_all(
+            send_b.at[0], recv_b.at[0], 3 + p, 3 + p, p * PART, PART,
+            extra=first_spread if p == 0 else None,
+        )
         send_input_grad(1, p * PART, PART)
     finish_left(1)
 
-    GROUP = 32
     groups = [(p, g) for p in range(2) for g in range(NB // GROUP)]
 
-    def pump(n):
+    def pump(n, extra=None):
         if n >= 2:
             p, g = groups[n - 2]
             await_block(send_f.at[0], a2a_send, 5 + n - 2, p * PART, PART, 2 * GROUP)
         if n < len(groups):
             p, g = groups[n]
-            all_to_all(send_f.at[0], recv_f.at[0], 5 + p, 5 + n, p * PART, PART, g * GROUP, GROUP)
+            all_to_all(send_f.at[0], recv_f.at[0], 5 + p, 5 + n, p * PART, PART, g * GROUP, GROUP, extra)
 
     await_block(recv_b.at[0], a2a_recv, 3, 0, PART)
     channel_back(0, recv_b.at[0], 0, 2)
-    gather_plane(1)
+    reduce_plane(1)
     pump(0)
     pump(1)
     await_block(recv_b.at[0], a2a_recv, 4, PART, PART)
-
-
-    def between():
-        gather_last(1)
-        pump(2)
-
-    channel_back(0, recv_b.at[0], 1, 2, between)
+    channel_back(0, recv_b.at[0], 1, 2, lambda: pump(2))
     reduce_siblings(0)
+    gather_plane(1)
     channel_out(0)
     reduce_first(0)
-    pump(3)
+    pump(3, first_burst)
     right_back(0, recv_b.at[0])
     reduce_plane(0)
-    pump(4)
-    pump(5)
+    gather_last(1, True)
+    pump(4, last_burst(0))
+    pump(5, last_burst(1))
     gather_plane(0)
     pump(6)
     pump(7)
@@ -554,27 +589,28 @@
         await_block(send_b.at[0], a2a_send, 3 + p, p * PART, PART)
     pump(8)
     pump(9)
-    pltpu.make_async_copy(gi_buf.at[0], gi_out.at[0], gi_loc).wait()
-    pltpu.make_async_copy(gi_buf.at[0], gi_out.at[0], gi_send).wait()
-    pltpu.make_async_copy(gi_buf.at[0], gi_out.at[0], gi_recv).wait()
+    pltpu.make_async_copy(gi_buf.at[0], gi_own, gi_loc).wait()
+    pltpu.make_async_copy(gi_buf.at[0], gi_own, gi_send).wait()
+    pltpu.make_async_copy(gi_buf.at[0], gi_own, gi_recv).wait()
 
 
 def body(x_saved, cotangent, seq_right, seq_left, chan_first, chan_second):
     v, dma = pltpu.VMEM, pltpu.SemaphoreType.DMA
     anywhere = pl.BlockSpec(memory_space=pl.ANY)
     vmem = pl.BlockSpec(memory_space=pltpu.VMEM)
-    gi, right, left, first, second = pl.pallas_call(
+    own, theirs, right, left, first, second = pl.pallas_call(
         kernel,
         name="monarch_backward",
         out_shape=[
-            jax.ShapeDtypeStruct((2, T, D), BF16),
+            jax.ShapeDtypeStruct((T, D), BF16),
+            jax.ShapeDtypeStruct((T, D), BF16),
             jax.ShapeDtypeStruct((T, T), F32),
             jax.ShapeDtypeStruct((T, T), F32),
-            jax.ShapeDtypeStruct((NK, NK, NK), F32),
-            jax.ShapeDtypeStruct((NK, NK, NK), F32),
+            jax.ShapeDtypeStruct((NK, NK, NK), BF16),
+            jax.ShapeDtypeStruct((NK, NK, NK), BF16),
         ],
         in_specs=[anywhere] * 6,
-        out_specs=[vmem] * 5,
+        out_specs=[anywhere] * 2 + [vmem] * 4,
         scratch_shapes=[
             v((2, T, D), BF16), v((2, T, T), BF16), v((2, T, T), BF16),
             v((2, D, NK), BF16), v((2, NK, NK, NK), BF16),
@@ -601,7 +637,12 @@
         chan_first[0].reshape(D, NK), chan_second[0],
     )
 
-    return (gi[None], right[None, None], left[None, None], first[None], second[None])
+    low = lax.axis_index("pipe") == 0
+    gi = jnp.stack([jnp.where(low, own, theirs), jnp.where(low, theirs, own)])
+    return (
+        gi[None], right[None, None], left[None, None],
+        first.astype(F32)[None], second.astype(F32)[None],
+    )
 
 
 def solution(mesh):

time: 143 us -> 138 us (0.965)
  local copies, waits for them, and re-layouts: 8.22 us -> 2.05 us
  other arithmetic: 0 us -> 5.65 us
  Pallas kernels: 134 us -> 129 us
    unnamed x13 -> x10, local copies, waits for them, and re-layouts: 8.22 us -> 2.05 us
    pallas_call x1, Pallas kernels: 134 us -> 129 us  [body(): pl.pallas_call(kernel, name='monarch_backward', out_shape=[jax.ShapeDtype...]
    broadcast_in_dim x0 -> x2, other arithmetic: none -> 3.97 us  [the longest x1 2.47 us: body(): second.astype(F32)[None]]
    another operation x0 -> x1, other arithmetic: none -> 1.68 us  [body(): gi = jnp.stack([jnp.where(low, own, theirs), jnp.where(low, theirs, own)])]
where the time goes in v5:
time: 138 us; the launch traced here: 137 us
  Pallas kernels  129 us (93%)
  other arithmetic  5.65 us (4%)
  local copies, waits for them, and re-layouts  2.05 us (1%)
    pallas_call x1, Pallas kernels, body(): pl.pallas_call(kernel, name='monarch_backward', out_shape=[jax.ShapeDtype...  129 us

profile of v5, /device:TPU:32, one launch (start us, length us, event | category | flops | bytes accessed | tf_op | source)
XLA Modules:
  0.0 137.2 jit_solution(12243073893934881326)
XLA Ops:
  0.6 128.9 %monarch_backward.1 = (bf16[128,4096]{1,0:T(8,128)(2,1)}, bf16[128,4096]{1,0:T(8,128)(2,1)}, f32[128,128]{1,0:T(8,128)}, f32[128,128]{1,0:T(8,128)}, bf16[64,64,...) custom-call(bf16[2,128,4096]{2,1,0:T(8,128)(2,1)} %bitcast.19, bf16[2,128,4096]{2,1,0:T(8,128)(2,1)} %cot_in.1, ...), custom_call_target="tpu_custom_call" | custom-call | tf_op jit(solution)/shard_map/monarch_backward/pallas_call | solution.py:601
  129.5 1.7 %select_bitcast_fusion.1 = (bf16[1,128,4096]{2,1,0:T(8,128)(2,1)S(1)}, bf16[1,128,4096]{2,1,0:T(8,128)(2,1)S(1)}) fusion(bf16[128,4096]{1,0:T(8,128)(2,1)} %get-tuple-element.11, bf16[128,4096]{1,0:T(8,128)(2,1)} %get-tuple-element.12, pred[]{:T(512)S(6)} %eq.3), kind=kLoop, calls=%fused_computation.4 | loop fusion | flops 1048576 | bytes 4194305 | tf_op jit(solution)/shard_map/stack | solution.py:641
  131.2 0.0 copy-start
  131.2 0.0 copy-start.1
  131.2 1.5 %maximum_bitcast_fusion = bf16[1,2,128,4096]{3,2,1,0:T(8,128)(2,1)} fusion(bf16[1,128,4096]{2,1,0:T(8,128)(2,1)S(1)} %get-tuple-element.18, bf16[1,128,4096]{2,1,0:T(8,128)(2,1)S(1)} %get-tuple-element.17), kind=kLoop, calls=%fused_computation | loop fusion | flops 1048576 | bytes 4194304 | tf_op jit(solution)/shard_map/broadcast_in_dim | solution.py:643
  132.7 0.0 copy-done
  132.7 0.8 copy-done.1
  133.5 0.0 copy-start.3
  133.5 0.0 copy-start.2
  133.5 2.5 %bitcast_convert_fusion = (f32[1,64,64,64]{3,2,1,0:T(8,128)}, f32[1,64,64,64]{3,2,1,0:T(8,128)}) fusion(bf16[64,64,64]{2,1,0:T(8,128)(2,1)S(1)} %copy-done.1, bf16[64,64,64]{2,1,0:T(8,128)(2,1)S(1)} %copy-done), kind=kLoop, calls=%fused_computation.1 | loop fusion | flops 524288 | bytes 3145728 | tf_op jit(solution)/shard_map/broadcast_in_dim | solution.py:644
  136.0 0.0 copy-done.3
  136.0 0.6 copy.13
  136.6 0.0 copy-done.2
  136.6 0.6 copy.14
Async XLA Ops:
  131.2 1.5 %copy-start = (bf16[64,64,64]{2,1,0:T(8,128)(2,1)S(1)}, bf16[64,64,64]{2,1,0:T(8,128)(2,1)}, u32[]{:S(2)}) copy-start(bf16[64,64,64]{2,1,0:T(8,128)(2,1)} %get-tuple-element.15) | copy-start | bytes 1572868
  131.2 2.3 %copy-start.1 = (bf16[64,64,64]{2,1,0:T(8,128)(2,1)S(1)}, bf16[64,64,64]{2,1,0:T(8,128)(2,1)}, u32[]{:S(2)}) copy-start(bf16[64,64,64]{2,1,0:T(8,128)(2,1)} %get-tuple-element.16) | copy-start | bytes 1572868
  133.5 2.5 %copy-start.3 = (f32[128,128]{1,0:T(8,128)S(1)}, f32[128,128]{1,0:T(8,128)}, u32[]{:S(2)}) copy-start(f32[128,128]{1,0:T(8,128)} %get-tuple-element.13) | copy-start | bytes 196612
  133.5 3.1 %copy-start.2 = (f32[128,128]{1,0:T(8,128)S(1)}, f32[128,128]{1,0:T(8,128)}, u32[]{:S(2)}) copy-start(f32[128,128]{1,0:T(8,128)} %get-tuple-element.14) | copy-start | bytes 196612

commit v6 on v5

--- a/solution.py
+++ b/solution.py
@@ -217,9 +217,8 @@
         lax.fori_loop(0, HALF // TILE, step, 0)
         fold(lr.at[section, 0])
 
-    def channel_back(section, returned, part, parts, between=lambda: None):
-        tiles = HALF // TILE // parts
-        pairs = NK // 4 // parts
+    def channel_back(section, returned, lo, size, between=None):
+        pairs = size // T
         first_half = lax.broadcasted_iota(jnp.int32, (NK, T), 1) < NK
 
         def step(i, carry):
@@ -227,7 +226,7 @@
             hg_buf[cs, :] = mm(returned[:, cs], rexp[section], 0, 0).astype(BF16)
             return carry
 
-        lax.fori_loop(part * tiles, (part + 1) * tiles, step, 0)
+        lax.fori_loop(lo // TILE, (lo + size) // TILE, step, 0)
 
         def pair(b, carry):
             for h in range(2):
@@ -243,10 +242,10 @@
                     mt_buf[k0 + q] = back.astype(BF16)
             return carry
 
-        lax.fori_loop(part * pairs, (part + 1) * pairs, pair, 0, unroll=2)
+        lax.fori_loop(lo // T, lo // T + pairs, pair, 0, unroll=2)
         for h in range(2):
-            swap_blocks(mt_buf, mg_view, h * (NK // 2) + part * 2 * pairs, 2 * pairs)
-        if part < parts - 1:
+            swap_blocks(mt_buf, mg_view, h * (NK // 2) + lo // NK, 2 * pairs)
+        if between is None:
             return
         between()
 
@@ -501,8 +500,10 @@
     build_pairs(other)
     forward(1, send_f.at[1])
     PART = HALF // 2
-    for p in range(2):
-        all_to_all(send_f.at[1], recv_f.at[1], 1 + p, 1 + p, p * PART, PART)
+    CUT = 2 * TILE
+    spans = ((0, CUT), (CUT, HALF - CUT))
+    for p, (lo, size) in enumerate(spans):
+        all_to_all(send_f.at[1], recv_f.at[1], 1 + p, 1 + p, lo, size)
 
     @pl.when(core == 1)
     def _():
@@ -511,22 +512,22 @@
     forward(0, send_f.at[0])
 
     await_block(recv_b.at[1], a2a_recv, 0, 0, HALF)
-    channel_back(1, recv_b.at[1], 0, 1)
+    channel_back(1, recv_b.at[1], 0, HALF, lambda: None)
     reduce_siblings(1)
     channel_out(1)
     reduce_first(1)
     right_back(1, recv_b.at[1])
 
     acc[...] = jnp.zeros_like(acc)
-    for p in range(2):
-        await_block(recv_f.at[1], a2a_recv, 1 + p, p * PART, PART)
-        carry_out(1, recv_f.at[1], gy_buf, p * PART, PART)
-        gate(0, gi_buf.at[1], send_b.at[0], p * PART, PART)
+    for p, (lo, size) in enumerate(spans):
+        await_block(recv_f.at[1], a2a_recv, 1 + p, lo, size)
+        carry_out(1, recv_f.at[1], gy_buf, lo, size)
+        gate(0, gi_buf.at[1], send_b.at[0], lo, size)
         all_to_all(
-            send_b.at[0], recv_b.at[0], 3 + p, 3 + p, p * PART, PART,
+            send_b.at[0], recv_b.at[0], 3 + p, 3 + p, lo, size,
             extra=first_spread if p == 0 else None,
         )
-        send_input_grad(1, p * PART, PART)
+        send_input_grad(1, lo, size)
     finish_left(1)
 
     groups = [(p, g) for p in range(2) for g in range(NB // GROUP)]
@@ -539,25 +540,25 @@
             p, g = groups[n]
             all_to_all(send_f.at[0], recv_f.at[0], 5 + p, 5 + n, p * PART, PART, g * GROUP, GROUP, extra)
 
-    await_block(recv_b.at[0], a2a_recv, 3, 0, PART)
-    channel_back(0, recv_b.at[0], 0, 2)
+    await_block(recv_b.at[0], a2a_recv, 3, 0, CUT)
+    channel_back(0, recv_b.at[0], 0, CUT)
     reduce_plane(1)
     pump(0)
     pump(1)
-    await_block(recv_b.at[0], a2a_recv, 4, PART, PART)
-    channel_back(0, recv_b.at[0], 1, 2, lambda: pump(2))
+    await_block(recv_b.at[0], a2a_recv, 4, CUT, HALF - CUT)
+    channel_back(0, recv_b.at[0], CUT, HALF - CUT, lambda: pump(2))
     reduce_siblings(0)
     gather_plane(1)
-    channel_out(0)
     reduce_first(0)
     pump(3, first_burst)
+    channel_out(0)
     right_back(0, recv_b.at[0])
     reduce_plane(0)
     gather_last(1, True)
-    pump(4, last_burst(0))
-    pump(5, last_burst(1))
+    pump(4)
+    pump(5, last_burst(0))
     gather_plane(0)
-    pump(6)
+    pump(6, last_burst(1))
     pump(7)
     acc[...] = jnp.zeros_like(acc)
     await_block(recv_f.at[0], a2a_recv, 5, 0, PART)
@@ -584,9 +585,9 @@
     for i in range(5):
         exchange_copy(i).wait_send()
     await_block(send_b.at[1], a2a_send, 0, 0, HALF)
-    for p in range(2):
-        await_block(send_f.at[1], a2a_send, 1 + p, p * PART, PART)
-        await_block(send_b.at[0], a2a_send, 3 + p, p * PART, PART)
+    for p, (lo, size) in enumerate(spans):
+        await_block(send_f.at[1], a2a_send, 1 + p, lo, size)
+        await_block(send_b.at[0], a2a_send, 3 + p, lo, size)
     pump(8)
     pump(9)
     pltpu.make_async_copy(gi_buf.at[0], gi_own, gi_loc).wait()

time: 138 us -> 138 us (level)
  no operation moved by 1% of the time
where the time goes in v6:
time: 138 us; the launch traced here: 137 us
  Pallas kernels  129 us (93%)
  other arithmetic  5.65 us (4%)
  local copies, waits for them, and re-layouts  2.05 us (1%)
    pallas_call x1, Pallas kernels, body(): pl.pallas_call(kernel, name='monarch_backward', out_shape=[jax.ShapeDtype...  129 us

profile of v6, /device:TPU:32, one launch (start us, length us, event | category | flops | bytes accessed | tf_op | source)
XLA Modules:
  0.0 137.0 jit_solution(6288498245129105373)
XLA Ops:
  0.6 128.7 %monarch_backward.1 = (bf16[128,4096]{1,0:T(8,128)(2,1)}, bf16[128,4096]{1,0:T(8,128)(2,1)}, f32[128,128]{1,0:T(8,128)}, f32[128,128]{1,0:T(8,128)}, bf16[64,64,...) custom-call(bf16[2,128,4096]{2,1,0:T(8,128)(2,1)} %bitcast.19, bf16[2,128,4096]{2,1,0:T(8,128)(2,1)} %cot_in.1, ...), custom_call_target="tpu_custom_call" | custom-call | tf_op jit(solution)/shard_map/monarch_backward/pallas_call | solution.py:602
  129.3 1.7 %select_bitcast_fusion.1 = (bf16[1,128,4096]{2,1,0:T(8,128)(2,1)S(1)}, bf16[1,128,4096]{2,1,0:T(8,128)(2,1)S(1)}) fusion(bf16[128,4096]{1,0:T(8,128)(2,1)} %get-tuple-element.11, bf16[128,4096]{1,0:T(8,128)(2,1)} %get-tuple-element.12, pred[]{:T(512)S(6)} %eq.3), kind=kLoop, calls=%fused_computation.4 | loop fusion | flops 1048576 | bytes 4194305 | tf_op jit(solution)/shard_map/stack | solution.py:642
  131.0 0.0 copy-start
  131.0 0.0 copy-start.1
  131.0 1.5 %maximum_bitcast_fusion = bf16[1,2,128,4096]{3,2,1,0:T(8,128)(2,1)} fusion(bf16[1,128,4096]{2,1,0:T(8,128)(2,1)S(1)} %get-tuple-element.18, bf16[1,128,4096]{2,1,0:T(8,128)(2,1)S(1)} %get-tuple-element.17), kind=kLoop, calls=%fused_computation | loop fusion | flops 1048576 | bytes 4194304 | tf_op jit(solution)/shard_map/broadcast_in_dim | solution.py:644
  132.5 0.0 copy-done
  132.5 0.8 copy-done.1
  133.3 0.0 copy-start.3
  133.3 0.0 copy-start.2
  133.3 2.5 %bitcast_convert_fusion = (f32[1,64,64,64]{3,2,1,0:T(8,128)}, f32[1,64,64,64]{3,2,1,0:T(8,128)}) fusion(bf16[64,64,64]{2,1,0:T(8,128)(2,1)S(1)} %copy-done.1, bf16[64,64,64]{2,1,0:T(8,128)(2,1)S(1)} %copy-done), kind=kLoop, calls=%fused_computation.1 | loop fusion | flops 524288 | bytes 3145728 | tf_op jit(solution)/shard_map/broadcast_in_dim | solution.py:645
  135.8 0.0 copy-done.3
  135.8 0.6 copy.13
  136.4 0.0 copy-done.2
  136.4 0.6 copy.14
Async XLA Ops:
  131.0 1.5 %copy-start = (bf16[64,64,64]{2,1,0:T(8,128)(2,1)S(1)}, bf16[64,64,64]{2,1,0:T(8,128)(2,1)}, u32[]{:S(2)}) copy-start(bf16[64,64,64]{2,1,0:T(8,128)(2,1)} %get-tuple-element.15) | copy-start | bytes 1572868
  131.0 2.3 %copy-start.1 = (bf16[64,64,64]{2,1,0:T(8,128)(2,1)S(1)}, bf16[64,64,64]{2,1,0:T(8,128)(2,1)}, u32[]{:S(2)}) copy-start(bf16[64,64,64]{2,1,0:T(8,128)(2,1)} %get-tuple-element.16) | copy-start | bytes 1572868
  133.3 2.5 %copy-start.3 = (f32[128,128]{1,0:T(8,128)S(1)}, f32[128,128]{1,0:T(8,128)}, u32[]{:S(2)}) copy-start(f32[128,128]{1,0:T(8,128)} %get-tuple-element.13) | copy-start | bytes 196612
  133.3 3.1 %copy-start.2 = (f32[128,128]{1,0:T(8,128)S(1)}, f32[128,128]{1,0:T(8,128)}, u32[]{:S(2)}) copy-start(f32[128,128]{1,0:T(8,128)} %get-tuple-element.14) | copy-start | bytes 196612
